TPU v7x, 256 devices: a whole 4x4x8 slice. The times are simulated.
256 devices in a mesh: seg: 32 (over y, x, core), fsdp: 8 (over z).
Axes of the slice: x: 4, y: 4, z: 8, core: 2. Of those that a mesh axis runs over, the one named last changes fastest.
Arguments:
- tokens: bfloat16 [8, 8192, 4096], P('fsdp', 'seg')
- w_query: bfloat16 [4096, 2048], P(('seg', 'fsdp'))
- w_key: bfloat16 [4096, 512], P(('seg', 'fsdp'))
- value_weight: bfloat16 [4096, 512], P(('seg', 'fsdp')), may hold values from -0.09375 to 0.09375
- gate_bias: float32 [16], replicated, may hold values from -2 to 2
- block_mask: int32 [8, 32, 2, 2], P('fsdp', 'seg'), may hold values from 0 to 1, as said below
- valid_len: int32 [8, 32], P('fsdp', 'seg'), may hold values from 1 to 256, as said below
Outputs:
- attended: bfloat16 [8, 8192, 2048], P('fsdp', 'seg')
Inputs may be any that keep to these rules, and one draw needn't show every extreme that they name: block_mask[b, s] is 1 on its diagonal, 0 above it, and 0 or 1 below it. `valid_len`: the first segment of every book is full.
All inputs are finite; a program needn't handle non-finite values.
Results may differ from a plain program's by a relative error of at most 0.0095.
Values may be sent and summed in bfloat16 or wider, within the bound.
A program may use at most 128 MiB of HBM per device.

v0:
```python
import jax
import jax.numpy as jnp
from jax import lax
from jax.sharding import PartitionSpec as P

HEAD_SIZE = 128
BLK = 128


def carried_in(array, axis, combine, identity):
    length, here = (lax.axis_size(axis), lax.axis_index(axis))
    everything = jax.tree.map(
        lambda part, kind: lax.all_gather(part.astype(kind), axis),
        array,
        (jnp.bfloat16, jnp.bfloat16),
    )
    start = jax.tree.map(
        lambda part, zero: jnp.broadcast_to(jnp.asarray(zero, part.dtype), part.shape),
        array,
        identity,
    )

    def lap(k, before):
        reached = k < here
        new = combine(
            before, jax.tree.map(lambda part, own: part[k].astype(own.dtype), everything, array)
        )
        return jax.tree.map(lambda a, b: jnp.where(reached, a, b), new, before)

    return lax.fori_loop(0, length, lap, start)


def sigma_plus(values):
    return jax.nn.elu(values) + 1.0


def segment_delta(keys, values, valid):
    length = keys.shape[0]
    heads_kv = keys.shape[1] // HEAD_SIZE
    live = (jnp.arange(length, dtype=jnp.int32) < valid)[:, None, None]
    sig_keys = jnp.where(
        live, sigma_plus(keys.reshape(length, heads_kv, HEAD_SIZE).astype(jnp.float32)), 0.0
    )
    delta_m = jnp.einsum(
        "jgd,jge->gde",
        sig_keys,
        values.reshape(length, heads_kv, HEAD_SIZE).astype(jnp.float32),
        precision=lax.Precision.HIGHEST,
    )
    delta_z = jnp.sum(sig_keys, axis=0)
    return (delta_m, delta_z)


def memory_before(keys, values, valid):
    delta_m, delta_z = segment_delta(keys, values, valid)

    def combine(earlier, later):
        return (earlier[0] + later[0], earlier[1] + later[1])

    identity = (jnp.zeros_like(delta_m), jnp.zeros_like(delta_z))
    memory, normalizer = carried_in((delta_m, delta_z), "seg", combine, identity)
    return (memory, normalizer)


def segment_output(queries, keys, values, gate_bias, mask_blocks, valid, memory, normalizer):
    length = queries.shape[0]
    heads_kv = memory.shape[0]
    group = queries.shape[1] // (heads_kv * HEAD_SIZE)
    nblocks = mask_blocks.shape[0]
    q_heads = queries.reshape(length, heads_kv, group, HEAD_SIZE)
    k_heads = keys.reshape(length, heads_kv, HEAD_SIZE)
    v_heads = values.reshape(length, heads_kv, HEAD_SIZE)
    scores = jnp.einsum(
        "igxd,jgd->gxij", q_heads, k_heads, preferred_element_type=jnp.float32
    ) * HEAD_SIZE ** (-0.5)
    full = jnp.broadcast_to(mask_blocks[:, None, :, None], (nblocks, BLK, nblocks, BLK)).reshape(
        length, length
    )
    pos = jnp.arange(length, dtype=jnp.int32)
    allowed = (full > 0) & (pos[None, :] <= pos[:, None]) & (pos[None, :] < valid)
    masked = jnp.where(allowed, scores, -1e30)
    top = jnp.max(masked, axis=-1, keepdims=True)
    expo = jnp.where(allowed, jnp.exp(masked - top), 0.0)
    total = jnp.maximum(jnp.sum(expo, axis=-1, keepdims=True), 1.0)
    weights = (expo / total).astype(jnp.bfloat16)
    local = jnp.einsum("gxij,jgd->igxd", weights, v_heads, preferred_element_type=jnp.float32)
    sig_q = sigma_plus(q_heads.astype(jnp.float32))
    numer = jnp.einsum("igxd,gde->igxe", sig_q, memory, precision=lax.Precision.HIGHEST)
    denom = jnp.einsum("igxd,gd->igx", sig_q, normalizer, precision=lax.Precision.HIGHEST) + 1.0
    gate = jax.nn.sigmoid(gate_bias).reshape(heads_kv, group)[None, :, :, None]
    mixed = gate * (numer / denom[..., None]) + (1.0 - gate) * local
    live = (pos < valid)[:, None, None, None]
    return jnp.where(live, mixed, 0.0).reshape(length, -1).astype(jnp.bfloat16)


def shards(tokens, w_query, w_key, value_weight, gate_bias, block_mask, valid_len):
    seg_tokens = tokens[0]
    mask_blocks = block_mask[0, 0]
    valid = valid_len[0, 0]

    def add_rows(piece):
        return jnp.dot(seg_tokens, piece, preferred_element_type=jnp.float32)

    q_sum = add_rows(lax.all_gather(w_query, ("seg", "fsdp"), axis=0, tiled=True))
    k_sum = add_rows(lax.all_gather(w_key, ("seg", "fsdp"), axis=0, tiled=True))
    v_sum = add_rows(lax.all_gather(value_weight, ("seg", "fsdp"), axis=0, tiled=True))
    keys = k_sum.astype(jnp.bfloat16)
    values = v_sum.astype(jnp.bfloat16)
    queries = q_sum.astype(jnp.bfloat16)
    memory, normalizer = memory_before(keys, values, valid)
    output = segment_output(
        queries, keys, values, gate_bias, mask_blocks, valid, memory, normalizer
    )
    return output[None]


def solution(mesh):
    in_specs = (
        P("fsdp", "seg", None),
        P(("seg", "fsdp"), None),
        P(("seg", "fsdp"), None),
        P(("seg", "fsdp"), None),
        P(),
        P("fsdp", "seg", None, None),
        P("fsdp", "seg"),
    )
    out_specs = P("fsdp", "seg", None)
    return jax.shard_map(shards, mesh=mesh, in_specs=in_specs, out_specs=out_specs, check_vma=False)
```

profile of v0, /device:TPU:1, one launch (start us, length us, event | category | flops | bytes accessed | tf_op | source)
XLA Modules:
  0.0 465.9 jit_solution(6795826982219625871)
XLA Ops:
  8.7 121.7 %all-gather.6.cloned.1.call-done = bf16[4096,512]{1,0:T(8,128)(2,1)} async-done(((bf16[16,512]{1,0:T(8,128)(2,1)}), bf16[4096,512]{1,0:T(8,128)(2,1)}) %all-gather.6.cloned.1.call-update) | async-done | bytes 4194320 | tf_op jit(solution)/shard_map/all_gather | solution.py:105
  130.4 3.6 fusion.42
  134.3 112.1 %all-gather.8.cloned.1.call-done = bf16[4096,512]{1,0:T(8,128)(2,1)} async-done(((bf16[16,512]{1,0:T(8,128)(2,1)}), bf16[4096,512]{1,0:T(8,128)(2,1)}) %all-gather.8.cloned.1.call-update) | async-done | bytes 4194320 | tf_op jit(solution)/shard_map/all_gather | solution.py:106
  246.4 3.4 fusion.28
  249.8 1.3 convolution_convert_fusion.1
  253.0 23.6 %all_gather.23 = bf16[32,4,128]{2,1,0:T(4,128)(2,1)S(1)} all-gather(bf16[1,4,128]{2,1,0:T(4,128)(2,1)S(1)} %bitcast.97), channel_id=1, replica_groups=mesh['seg'=32,'fsdp'=8] {'seg'}, dimensions={0}, use_global_device_ids=true | all-gather | bytes 33792 | tf_op jit(solution)/shard_map/all_gather | solution.py:13
  276.7 22.9 %all-gather.12.cloned.1.call-done = bf16[128,128,128]{2,1,0:T(8,128)(2,1)} async-done(((bf16[4,128,128]{2,1,0:T(8,128)(2,1)}), bf16[128,128,128]{2,1,0:T(8,128)(2,1)}) %all-gather.12.cloned.1.call-update) | async-done | bytes 4194320 | tf_op jit(solution)/shard_map/all_gather | solution.py:13
  299.6 34.6 %while.16 = (s32[]{:T(128)}, f32[4,128,128]{2,1,0:T(8,128)S(1)}, f32[4,128]{1,0:T(4,128)S(1)}, s32[]{:T(128)}, bf16[32,4,128,128]{3,2,1,0:T(8,128)(2,1)}, /*inde...) while((s32[]{:T(128)}, f32[4,128,128]{2,1,0:T(8,128)S(1)}, f32[4,128]{1,0:T(4,128)S(1)}, ...), condition=%wide.region_2.3_spmd.clone, body=%wide.region_1.2_spmd.clone.sunk | while | flops 264196 | bytes 660603 | solution.py:30
  300.7 1.0 add_select_fusion.4
  301.8 1.0 add_select_fusion.4
  302.9 1.0 add_select_fusion.4
  303.9 1.0 add_select_fusion.4
  308.3 1.0 add_select_fusion.4
  310.4 1.0 add_select_fusion.4
  313.7 1.0 add_select_fusion.4
  314.8 1.0 add_select_fusion.4
  315.9 1.0 add_select_fusion.4
  318.0 1.0 add_select_fusion.4
  320.2 1.0 add_select_fusion.4
  325.6 1.0 add_select_fusion.4
  326.7 1.0 add_select_fusion.4
  328.9 1.0 add_select_fusion.4
  331.0 1.0 add_select_fusion.4
  334.2 93.2 %all-gather.10.cloned.1.call-done = bf16[4096,2048]{1,0:T(8,128)(2,1)} async-done(((bf16[16,2048]{1,0:T(8,128)(2,1)}), bf16[4096,2048]{1,0:T(8,128)(2,1)}) %all-gather.10.cloned.1.call-update) | async-done | bytes 16777232 | tf_op jit(solution)/shard_map/all_gather | solution.py:104
  427.4 9.2 %convolution_convert_fusion = bf16[256,2048]{1,0:T(8,128)(2,1)} fusion(bf16[4096,2048]{1,0:T(8,128)(2,1)} %all-gather.10.cloned.1.call-done, bf16[1,256,4096]{2,1,0:T(8,128)(2,1)S(1)} %copy-done), kind=kOutput, calls=%fused_computation.9 | convolution fusion | flops 4295491584 | bytes 19922944 | tf_op jit(solution)/shard_map/dot_general | solution.py:102
  436.6 1.5 copy.54
  438.1 5.2 %fusion.20 = f32[4,1,256,4]{1,2,3,0:T(8,128)} fusion(f32[4,128,1,1]{1,2,3,0:T(1,128)S(1)} %bitcast.96, bf16[256,4,4,128]{0,3,2,1:T(8,128)(2,1)S(1)} %bitcast.88), kind=kOutput, calls=%fused_computation.32 | convolution fusion | flops 8916992 | bytes 1067008 | tf_op jit(solution)/shard_map/igxd,gd->igx/dot_general | solution.py:89
  443.3 2.2 copy.57
  445.5 4.7 %fusion.69 = (f32[4,4,256]{2,1,0:T(4,128)S(1)}, f32[4,4,256,256]{2,3,1,0:T(8,128)}) fusion(pred[256,256]{0,1:T(8,128)(4,1)S(1)} %copy.35, bf16[256,4,4,128]{0,3,2,1:T(8,128)(2,1)S(1)} %bitcast.89, bf16[256,4,128,1]{2,1,0,3:T(4,128)(2,1)} %bitcast.92), kind=kOutput, calls=%fused_computation.76 | convolution fusion | flops 273678592 | bytes 5586944 | tf_op jit(solution)/shard_map/sub | solution.py:83
  450.2 2.8 fusion.14
  453.1 4.1 fusion.5
  457.1 2.3 copy.40
  (80 shorter events, 21.8 us)
Async XLA Ops:
  6.5 123.8 %copy-start = (bf16[1,256,4096]{2,1,0:T(8,128)(2,1)S(1)}, bf16[1,256,4096]{2,1,0:T(8,128)(2,1)}, u32[]{:S(2)}) copy-start(bf16[1,256,4096]{2,1,0:T(8,128)(2,1)} %param.9) | copy-start | bytes 6291460
  6.5 123.8 %all-gather.6.cloned.1.call-start = ((), (), s32[]{:S(2)}) async-start(), calls=%async_computation | async-start | bytes 4210688 | tf_op jit(solution)/shard_map/all_gather | solution.py:105
  7.3 239.1 %all-gather.8.cloned.1.call-start = ((), (), s32[]{:S(2)}) async-start(), calls=%async_computation.1 | async-start | bytes 4210688 | tf_op jit(solution)/shard_map/all_gather | solution.py:106
  8.0 291.6 %all-gather.12.cloned.1.call-start = ((), (), s32[]{:S(2)}) async-start(), calls=%async_computation.3 | async-start | bytes 4325376 | tf_op jit(solution)/shard_map/all_gather | solution.py:13
  134.1 115.7 %copy-start.1 = (bf16[256,4,128]{2,1,0:T(4,128)(2,1)}, bf16[256,4,128]{2,1,0:T(4,128)(2,1)S(1)}, u32[]{:S(2)}) copy-start(bf16[256,4,128]{2,1,0:T(4,128)(2,1)S(1)} %reshape.73) | copy-start | bytes 786436
  134.3 117.5 %copy-start.3 = (f32[16]{0:T(128)S(1)}, f32[16]{0:T(128)}, u32[]{:S(2)}) copy-start(f32[16]{0:T(128)} %param.13) | copy-start | bytes 196
  134.3 117.6 %copy-start.2 = (s32[1,1,2,2]{3,2,1,0:T(2,128)S(1)}, s32[1,1,2,2]{3,2,1,0:T(2,128)}, u32[]{:S(2)}) copy-start(s32[1,1,2,2]{3,2,1,0:T(2,128)} %param.14) | copy-start | bytes 52
  251.1 176.3 %all-gather.10.cloned.1.call-start = ((), (), s32[]{:S(2)}) async-start(), calls=%async_computation.2 | async-start | bytes 16842752 | tf_op jit(solution)/shard_map/all_gather | solution.py:104
Sparse Core Ops, SparseCore 0:
  11.0 119.3 all-gather.5
  134.0 112.3 all-gather.7
  251.3 48.3 all-gather.11
  303.1 124.3 all-gather.9
where the time goes:
time: 467 us; the launch traced here: 466 us
  waiting for transfers between devices  352 us (75%)
  matrix products  34.3 us (7%)
  other arithmetic  33.9 us (7%)
  blocking collectives  23.6 us (5%)
  between operations  13.9 us (3%)
  local copies, waits for them, and re-layouts  7.38 us (2%)
    all_gather x1, waiting for transfers between devices, shards(): k_sum = add_rows(lax.all_gather(w_key, ('seg', 'fsdp'), axis=0, tiled=True))  122 us
    all_gather x1, waiting for transfers between devices, shards(): lax.all_gather(value_weight, ('seg', 'fsdp'), axis=0, tiled=True)  112 us
    all_gather x1, waiting for transfers between devices, shards(): lax.all_gather(w_query, ('seg', 'fsdp'), axis=0, tiled=True)  93.2 us
    select_n x64, other arithmetic, lap(): return jax.tree.map(lambda a, b: jnp.where(reached, a, b), new, before)  33.8 us
    all_gather x1, blocking collectives, carried_in(): lax.all_gather(part.astype(kind), axis)  23.6 us
    all_gather x1, waiting for transfers between devices, carried_in(): lax.all_gather(part.astype(kind), axis)  22.9 us
    dot_general x3, matrix products, add_rows(): return jnp.dot(seg_tokens, piece, preferred_element_type=jnp.float32)  16.3 us
  transfers between devices with their start and end apart: 4, of which 4 were waited for; matrix products, arithmetic and copies ran while one was open for 8% of the time, Pallas kernels for 0%

commit v1 on v0

v1 whole, which is shorter than its diff:
```python
import functools

import jax
import jax.numpy as jnp
from jax import lax
from jax.experimental import pallas as pl
from jax.experimental.pallas import tpu as pltpu
from jax.sharding import PartitionSpec as P

HEAD = 128
SEG = 256
CW = 256
NCH = 6
ORDERS = (("x", "y", "z"), ("y", "z", "x"), ("z", "x", "y"))
MESH_ID = pl.DeviceIdType.MESH
F32 = jnp.float32
BF16 = jnp.bfloat16

PROGRAM = (
    [(c, 0) for c in (0, 1, 2)]
    + [(c, 1) for c in (0, 1, 2)]
    + [(c, 2) for c in (0, 1, 2)]
    + [(2, 3), (0, 3), (1, 3), (2, 4), (0, 4), (1, 4)]
    + [(c, 0) for c in (3, 4, 5)]
    + [(2, 5), (1, 5)]
    + [(c, 1) for c in (3, 4, 5)]
    + [(2, 6), (1, 6)]
    + [(c, 2) for c in (3, 4, 5)]
    + [(0, 5)]
    + [(5, 3), (4, 3), (3, 3), (5, 4), (4, 4), (5, 5), (4, 5)]
    + [(0, 6), (2, 7), (5, 6), (1, 7), (4, 6), (0, 7), (3, 4), (0, 8)]
    + ["keys", (1, 8), "values", "delta", (2, 8), (3, 5), "q0", (3, 6), "rows"]
    + [(4, 7), (5, 7), (3, 7), "memory", "a0", (3, 8), "q1", "a1", (4, 8), "q2", "a2", (5, 8), "q3", "a3"]
)


def sigma(v):
    return jnp.where(v > 0, v, jnp.exp(jnp.minimum(v, 0.0)) - 1.0) + 1.0


def body(
    dims,
    tok_hbm, wq_hbm, wk_hbm, wv_hbm, gate_ref, mask_ref, valid_ref,
    out_hbm,
    w, tok, acc, kbuf, vbuf, qbuf, meta, own, rx, ry, mem, stage,
    recv, send, csem_l, csem_s, csem_r, dsem_s, dsem_r, osem_l, osem_s, osem_r,
):
    seg = lax.axis_index("seg")
    z = lax.axis_index("fsdp")
    c = lax.rem(seg, 2)
    x = lax.rem(seg // 2, dims["x"])
    y = seg // (2 * dims["x"])
    pos = {"x": x, "y": y, "z": z}

    def device(xx, yy, cc, zz):
        return {"seg": (yy * dims["x"] + xx) * 2 + cc, "fsdp": zz}

    def shifted(dim, delta):
        at = dict(pos)
        at[dim] = lax.rem(pos[dim] + delta + dims[dim], dims[dim])
        return device(at["x"], at["y"], c, at["z"])

    sibling = device(x, y, 1 - c, z)

    barrier = pltpu.get_barrier_semaphore()
    peers = [sibling, shifted("z", 1), shifted("z", -1)]
    for dim in "xy":
        peers += [shifted(dim, k) for k in range(1, dims[dim])]
    for peer in peers:
        pl.semaphore_signal(barrier, inc=1, device_id=peer, device_id_type=MESH_ID)
    pl.semaphore_wait(barrier, len(peers))

    locals_, sends_, recvs_ = [], [], []

    def columns(ch, core):
        if ch < 2:
            return (wk_hbm, wv_hbm)[ch].at[:, pl.ds(pl.multiple_of(core * CW, CW), CW)]
        return wq_hbm.at[:, pl.ds(pl.multiple_of(core * 4 * CW + (ch - 2) * CW, CW), CW)]

    for ch in range(NCH):
        slot = w.at[ch, y, x, c, z]
        other = w.at[ch, y, x, 1 - c, z]
        there = pltpu.make_async_remote_copy(
            columns(ch, 1 - c), slot, csem_s.at[ch], csem_r.at[ch], device_id=sibling, device_id_type=MESH_ID
        )
        there.start()
        here = pltpu.make_async_copy(columns(ch, c), slot, csem_l.at[ch])
        here.start()
        back = pltpu.make_async_remote_copy(
            other, other, csem_s.at[ch], csem_r.at[ch], device_id=sibling, device_id_type=MESH_ID
        )
        locals_.append(here)
        sends_.append(there)
        recvs_.append(back)

    row8 = lax.broadcasted_iota(jnp.int32, (8, HEAD), 0)
    meta[c] = jnp.where(row8 == 0, valid_ref[0, 0], mask_ref[1, 0])
    meta_copy = pltpu.make_async_remote_copy(
        meta.at[c], meta.at[c], csem_s.at[NCH], csem_r.at[NCH], device_id=sibling, device_id_type=MESH_ID
    )
    meta_back = pltpu.make_async_remote_copy(
        meta.at[1 - c], meta.at[1 - c], csem_s.at[NCH], csem_r.at[NCH], device_id=sibling, device_id_type=MESH_ID
    )
    tok_copy = pltpu.make_async_remote_copy(
        tok_hbm, tok.at[c], csem_s.at[NCH + 1], csem_r.at[NCH + 1], device_id=sibling, device_id_type=MESH_ID
    )
    tok_back = pltpu.make_async_remote_copy(
        tok.at[1 - c], tok.at[1 - c], csem_s.at[NCH + 1], csem_r.at[NCH + 1], device_id=sibling, device_id_type=MESH_ID
    )
    tok_here = pltpu.make_async_copy(tok_hbm, tok.at[c], csem_l.at[NCH])

    def block(ch, order, stage_no, index, half):
        cols = slice(None) if half is None else pl.ds(half * (CW // 2), CW // 2)
        at = {d: pl.ds(pos[d], 1) for d in "xyz"}
        for d in order[:stage_no]:
            at[d] = slice(None)
        at[order[stage_no]] = pl.ds(index, 1)
        return w.at[ch, at["y"], at["x"], :, at["z"], :, cols]

    steps = {}
    for ch in range(NCH):
        order = ORDERS[ch % 3]
        steps[ch] = [(s, k) for s in range(3) for k in range(1, dims[order[s]] // 2 + 1)]

    def ring(ch, number, arriving):
        order = ORDERS[ch % 3]
        s, k = steps[ch][number]
        dim = order[s]
        n = dims[dim]
        copies = []
        for side, delta in ((0, 1), (1, -1)):
            back = k if arriving else k - 1
            index = lax.rem(pos[dim] - delta * back + n, n)
            half = side if 2 * k == n else None
            piece = block(ch, order, s, index, half)
            copies.append(
                pltpu.make_async_remote_copy(
                    piece, piece, send.at[ch, number, side], recv.at[ch, number, side],
                    device_id=shifted(dim, delta), device_id_type=MESH_ID,
                )
            )
        return copies

    sent = []

    def tick(ch, number):
        arrived = ring(ch, number - 1, True) if number else None
        leaving = ring(ch, number, False) if number < len(steps[ch]) else None
        if number == 0:
            locals_[ch].wait()
            recvs_[ch].wait_recv()
        same_stage = leaving is not None and number and steps[ch][number][0] == steps[ch][number - 1][0]
        if same_stage:
            for a, b in zip(arrived, leaving):
                a.wait_recv()
                b.start()
        else:
            if arrived is not None:
                for a in arrived:
                    a.wait_recv()
            if leaving is not None:
                for b in leaving:
                    b.start()
        if leaving is not None:
            sent.extend(leaving)

    def project(ch, dst):
        def part(i, first):
            a = tok[:, :, pl.ds(pl.multiple_of(i * 1024, 1024), 1024)].reshape(2 * SEG, 1024)
            b = w[ch, i].reshape(1024, CW)
            r = jnp.dot(a, b, preferred_element_type=F32)
            if first:
                acc[...] = r
            else:
                acc[...] += r

        part(0, True)

        @pl.loop(1, dims["y"])
        def _(i):
            part(i, False)

        dst[...] = acc[...].astype(BF16).reshape(2, SEG, CW)

    def delta():
        jrow = lax.broadcasted_iota(jnp.int32, (SEG, HEAD), 0)
        for g in range(2):
            cols = slice(g * HEAD, (g + 1) * HEAD)
            both = []
            for s in range(2):
                live = jrow < meta[s, 0:1, :]
                sig = jnp.where(live, sigma(kbuf[s, :, cols].astype(F32)), 0.0)
                zrow = jnp.sum(sig, axis=0, keepdims=True)
                m = lax.dot_general(
                    sig.astype(BF16), vbuf[s, :, cols], (((0,), (0,)), ((), ())), preferred_element_type=F32
                )
                both.append((m, zrow))
            own[g, 0:HEAD, :] = both[0][0]
            own[g, HEAD : HEAD + 16, :] = jnp.broadcast_to(both[0][1], (16, HEAD))
            rx[x, g, 0:HEAD, :] = (both[0][0] + both[1][0]).astype(BF16)
            rx[x, g, HEAD : HEAD + 16, :] = jnp.broadcast_to(both[0][1] + both[1][1], (16, HEAD)).astype(BF16)

    def exchange(dim, buf, number, arriving):
        n = dims[dim]
        copies = []
        for k in range(1, n):
            index = lax.rem(pos[dim] - k + n, n) if arriving else pos[dim]
            copies.append(
                pltpu.make_async_remote_copy(
                    buf.at[index], buf.at[index], dsem_s.at[number, k - 1], dsem_r.at[number, k - 1],
                    device_id=shifted(dim, k), device_id_type=MESH_ID,
                )
            )
        return copies

    def launch(copies):
        for one in copies:
            one.start()
        sent.extend(copies)

    def row_totals():
        for one in exchange("x", rx, 0, True):
            one.wait_recv()
        for g in range(2):
            total = jnp.zeros((HEAD + 16, HEAD), F32)
            for k in range(dims["x"]):
                total = total + rx[k, g].astype(F32)
            ry[y, g] = total.astype(BF16)
        launch(exchange("y", ry, 1, False))

    def memory():
        for one in exchange("y", ry, 1, True):
            one.wait_recv()
        for g in range(2):
            total = jnp.zeros((HEAD + 16, HEAD), F32)
            for k in range(dims["x"]):
                total = total + jnp.where(k < x, rx[k, g].astype(F32), 0.0)
            for k in range(dims["y"]):
                total = total + jnp.where(k < y, ry[k, g].astype(F32), 0.0)
            for s in range(2):
                if s:
                    total = total + own[g]
                mem[s, g, :, 0:HEAD] = total[0:HEAD].astype(BF16)
                zcol = jnp.transpose(jnp.broadcast_to(total[HEAD : HEAD + 1], (HEAD, HEAD)))
                mem[s, g, :, HEAD:] = zcol.astype(BF16)

    ones = jnp.ones((SEG, HEAD), BF16)

    def attend(j):
        g = j // 2
        kcols = slice(g * HEAD, (g + 1) * HEAD)
        gates = []
        for e in range(2):
            bias = jnp.full((1, HEAD), gate_ref[c * 8 + 2 * j + e], F32)
            gates.append(jax.nn.sigmoid(bias))
        for s in range(2):
            valid = meta[s, 0:1, :]
            for r in range(2):
                nk = (r + 1) * HEAD
                rows = slice(r * HEAD, (r + 1) * HEAD)
                q = jnp.concatenate([qbuf[j, s, rows, 0:HEAD], qbuf[j, s, rows, HEAD:]], axis=0)
                keys = kbuf[s, 0:nk, kcols]
                vals = jnp.concatenate([vbuf[s, 0:nk, kcols], ones[0:nk]], axis=1)
                scores = lax.dot_general(q, keys, (((1,), (1,)), ((), ())), preferred_element_type=F32)
                irow = lax.broadcasted_iota(jnp.int32, (HEAD, nk), 0) + r * HEAD
                jcol = lax.broadcasted_iota(jnp.int32, (HEAD, nk), 1)
                wide = valid if r == 0 else jnp.concatenate([valid, valid], axis=1)
                allowed = (jcol <= irow) & (jcol < wide)
                if r:
                    lower = jnp.concatenate([meta[s, 1:2, :], jnp.ones((1, HEAD), jnp.int32)], axis=1)
                    allowed = allowed & (lower > 0)
                allowed = jnp.concatenate([allowed, allowed], axis=0)
                masked = jnp.where(allowed, scores, -1e30)
                top = jnp.max(masked, axis=1, keepdims=True)
                expo = jnp.where(allowed, jnp.exp((masked - top) * HEAD**-0.5), 0.0).astype(BF16)
                local = jnp.dot(expo, vals, preferred_element_type=F32)
                total = jnp.maximum(local[:, HEAD:], 1.0)
                sq = sigma(q.astype(F32)).astype(BF16)
                retrieved = jnp.dot(sq, mem[s, g], preferred_element_type=F32)
                remembered = retrieved[:, 0:HEAD] / (retrieved[:, HEAD:] + 1.0)
                local = local[:, 0:HEAD] / total
                alive = (lax.broadcasted_iota(jnp.int32, (HEAD, HEAD), 0) + r * HEAD) < valid
                for e in range(2):
                    half = slice(e * HEAD, (e + 1) * HEAD)
                    mixed = gates[e] * remembered[half] + (1.0 - gates[e]) * local[half]
                    stage[j, s, rows, half] = jnp.where(alive, mixed, 0.0).astype(BF16)
        place = pl.ds(pl.multiple_of(c * 4 * CW + j * CW, CW), CW)
        there = pltpu.make_async_remote_copy(
            stage.at[j, 1 - c], out_hbm.at[:, place], osem_s.at[j], osem_r.at[j], device_id=sibling, device_id_type=MESH_ID
        )
        there.start()
        here = pltpu.make_async_copy(stage.at[j, c], out_hbm.at[:, place], osem_l.at[j])
        here.start()
        finals.append((there, here))

    finals = []
    for item in PROGRAM:
        if item == "keys":
            tok_here.wait()
            tok_back.wait_recv()
            project(0, kbuf)
        elif item == "values":
            project(1, vbuf)
        elif item == "delta":
            meta_back.wait_recv()
            delta()
            launch(exchange("x", rx, 0, False))
        elif item == "rows":
            row_totals()
        elif item == "memory":
            memory()
        elif item[0] == "q":
            project(2 + int(item[1]), qbuf.at[int(item[1])])
        elif item[0] == "a":
            attend(int(item[1]))
        else:
            tick(*item)
            if item == (2, 0):
                meta_copy.start()
                tok_copy.start()
                tok_here.start()

    for j, (there, here) in enumerate(finals):
        here.wait()
        there.wait_send()
        arriving = out_hbm.at[:, pl.ds(pl.multiple_of((1 - c) * 4 * CW + j * CW, CW), CW)]
        pltpu.make_async_remote_copy(
            stage.at[j, 1 - c], arriving, osem_s.at[j], osem_r.at[j], device_id=sibling, device_id_type=MESH_ID
        ).wait_recv()
    for one in sent + sends_ + [meta_copy, tok_copy]:
        one.wait_send()


def solution(mesh):
    segs, nz = mesh.shape["seg"], mesh.shape["fsdp"]
    side = {32: 4, 8: 2, 16: 4}[segs]
    dims = {"x": side, "y": segs // 2 // side, "z": nz}

    def shards(tokens, w_query, w_key, value_weight, gate_bias, block_mask, valid_len):
        hbm = pl.BlockSpec(memory_space=pltpu.HBM)
        smem = pl.BlockSpec(memory_space=pltpu.SMEM)
        x, y, nz = dims["x"], dims["y"], dims["z"]
        dma = pltpu.SemaphoreType.DMA
        out = pl.pallas_call(
            functools.partial(body, dims),
            out_shape=jax.ShapeDtypeStruct((SEG, 2048), BF16),
            in_specs=[hbm] * 4 + [smem] * 3,
            out_specs=hbm,
            scratch_shapes=[
                pltpu.VMEM((NCH, y, x, 2, nz, 16, CW), BF16),
                pltpu.VMEM((2, SEG, 4096), BF16),
                pltpu.VMEM((2 * SEG, CW), F32),
                pltpu.VMEM((2, SEG, CW), BF16),
                pltpu.VMEM((2, SEG, CW), BF16),
                pltpu.VMEM((4, 2, SEG, CW), BF16),
                pltpu.VMEM((2, 8, HEAD), jnp.int32),
                pltpu.VMEM((2, HEAD + 16, HEAD), F32),
                pltpu.VMEM((x, 2, HEAD + 16, HEAD), BF16),
                pltpu.VMEM((y, 2, HEAD + 16, HEAD), BF16),
                pltpu.VMEM((2, 2, HEAD, 2 * HEAD), BF16),
                pltpu.VMEM((4, 2, SEG, CW), BF16),
                dma((NCH, 8, 2)),
                dma((NCH, 8, 2)),
                dma((NCH + 1,)),
                dma((NCH + 2,)),
                dma((NCH + 2,)),
                dma((2, 3)),
                dma((2, 3)),
                dma((4,)),
                dma((4,)),
                dma((4,)),
            ],
            compiler_params=pltpu.CompilerParams(
                collective_id=0, has_side_effects=True, vmem_limit_bytes=56 * 1024 * 1024
            ),
        )(tokens[0], w_query, w_key, value_weight, gate_bias, block_mask[0, 0], valid_len)
        return out[None]

    in_specs = (
        P("fsdp", "seg", None),
        P(("seg", "fsdp"), None),
        P(("seg", "fsdp"), None),
        P(("seg", "fsdp"), None),
        P(),
        P("fsdp", "seg", None, None),
        P("fsdp", "seg"),
    )
    return jax.shard_map(
        shards, mesh=mesh, in_specs=in_specs, out_specs=P("fsdp", "seg", None), check_vma=False
    )
```

time: 467 us -> 104 us (0.22)
  waiting for transfers between devices: 352 us -> 0 us
  Pallas kernels: 0 us -> 101 us
  matrix products: 34.3 us -> 0 us
  other arithmetic: 33.9 us -> 0 us
  blocking collectives: 23.6 us -> 0 us
  between operations: 13.9 us -> 0.66 us
  local copies, waits for them, and re-layouts: 7.38 us -> 2.3 us
    all_gather x4 -> x0, waiting for transfers between devices: 350 us -> none  [the longest x1 122 us: shards(): k_sum = add_rows(lax.all_gather(w_key, ('seg', 'fsdp'), axis=0, tiled=True))]
    pallas_call x0 -> x1, Pallas kernels: none -> 101 us  [shards(): pl.pallas_call(functools.partial(body, dims), out_shape=jax.ShapeDtypeStr...]
    select_n x64 -> x0, other arithmetic: 33.8 us -> none  [lap(): return jax.tree.map(lambda a, b: jnp.where(reached, a, b), new, before)]
    dot_general x7 -> x0, matrix products: 29.6 us -> none  [the longest x3 16.3 us: add_rows(): return jnp.dot(seg_tokens, piece, preferred_element_type=jnp.float32)]
    all_gather x1 -> x0, blocking collectives: 23.6 us -> none  [carried_in(): lax.all_gather(part.astype(kind), axis)]
    sub x1 -> x0, matrix products: 4.7 us -> none  [segment_output(): expo = jnp.where(allowed, jnp.exp(masked - top), 0.0)]
  transfers between devices with their start and end apart: 4 -> 0, of which waited for: 4 -> 0; matrix products, arithmetic and copies ran while one was open for 8% -> 0% of each run, Pallas kernels for 0% -> 0%
where the time goes in v1:
time: 104 us; the launch traced here: 103 us
  Pallas kernels  101 us (97%)
  local copies, waits for them, and re-layouts  2.3 us (2%)
    pallas_call x1, Pallas kernels, shards(): pl.pallas_call(functools.partial(body, dims), out_shape=jax.ShapeDtypeStr...  101 us
    unnamed x1, local copies, waits for them, and re-layouts  2.3 us

profile of v1, /device:TPU:1, one launch (start us, length us, event | category | flops | bytes accessed | tf_op | source)
XLA Modules:
  0.0 103.5 jit_solution(14163360952535468274)
XLA Ops:
  0.7 100.5 %shard_map.73 = bf16[256,2048]{1,0:T(8,128)(2,1)} custom-call(bf16[256,4096]{1,0:T(8,128)(2,1)} %bitcast.4, bf16[16,2048]{1,0:T(8,128)(2,1)} %wq_hbm.1, bf16[16,512]{1,0:T(8,128)(2,1)} %wk_hbm.1, bf16[16,512]{1,0:T(8,128)(2,1)} %wv_hbm.1, f32[16]{0:T(128)} %gate_ref.1, s32[2,2]{1,0:T(2,128)} %bitcast.5, s32[1,1]{1,0:T(1,128)S(6)} %copy.9.valid_ref), custom_call_target="tpu_custom_call" | custom-call | tf_op jit(solution)/shard_map/pallas_call | solution.py:344
  101.2 2.3 %copy.10 = bf16[1,256,2048]{2,1,0:T(8,128)(2,1)} copy(bf16[1,256,2048]{2,1,0:T(8,128)(2,1)} %bitcast.3) | data formatting | bytes 2097152

commit v2 on v1

--- a/solution.py
+++ b/solution.py
@@ -10,27 +10,22 @@
 HEAD = 128
 SEG = 256
 CW = 256
-NCH = 6
-ORDERS = (("x", "y", "z"), ("y", "z", "x"), ("z", "x", "y"))
+NCH = 12
+ORDERS = ("xyz", "zyx", "zxy", "yxz", "zyx", "zxy")
+DIRECT, RING = "direct", "ring"
+KINDS = (DIRECT, DIRECT, RING)
 MESH_ID = pl.DeviceIdType.MESH
 F32 = jnp.float32
 BF16 = jnp.bfloat16
 
 PROGRAM = (
-    [(c, 0) for c in (0, 1, 2)]
-    + [(c, 1) for c in (0, 1, 2)]
-    + [(c, 2) for c in (0, 1, 2)]
-    + [(2, 3), (0, 3), (1, 3), (2, 4), (0, 4), (1, 4)]
-    + [(c, 0) for c in (3, 4, 5)]
-    + [(2, 5), (1, 5)]
-    + [(c, 1) for c in (3, 4, 5)]
-    + [(2, 6), (1, 6)]
-    + [(c, 2) for c in (3, 4, 5)]
-    + [(0, 5)]
-    + [(5, 3), (4, 3), (3, 3), (5, 4), (4, 4), (5, 5), (4, 5)]
-    + [(0, 6), (2, 7), (5, 6), (1, 7), (4, 6), (0, 7), (3, 4), (0, 8)]
-    + ["keys", (1, 8), "values", "delta", (2, 8), (3, 5), "q0", (3, 6), "rows"]
-    + [(4, 7), (5, 7), (3, 7), "memory", "a0", (3, 8), "q1", "a1", (4, 8), "q2", "a2", (5, 8), "q3", "a3"]
+    (0, 0), (1, 0), (2, 0), (3, 0), (4, 0), (5, 0), (6, 0), (7, 0), (0, 1), (8, 0), (9, 0), (10, 0), (3, 1),
+    (11, 0), (1, 1), (6, 1), (2, 1), (4, 1), (9, 1), (0, 2), (5, 1), (3, 2), (7, 1), (1, 2), (8, 1), (10, 1),
+    (2, 2), (11, 1), (4, 2), (0, 3), (5, 2), (3, 3), (0, 4), (1, 3), (7, 2), (3, 4), (2, 3), (8, 2), (0, 5),
+    (6, 2), (3, 5), (9, 2), (5, 3), (11, 2), (0, 6), (4, 3), (10, 2), (6, 3), (3, 6), (1, 4), "keys", (2, 4),
+    "values", "delta", (9, 3), (6, 4), (5, 4), (7, 3), (8, 3), (9, 4), (4, 4), "q0", (6, 5), "rows", (11, 3),
+    (9, 5), (10, 3), (6, 6), "memory", "a0", (7, 4), "q1", "a1", (8, 4), (9, 6), "q2", "a2", (11, 4), (10, 4),
+    "q3", "a3",
 )
 
 
@@ -42,7 +37,7 @@
     dims,
     tok_hbm, wq_hbm, wk_hbm, wv_hbm, gate_ref, mask_ref, valid_ref,
     out_hbm,
-    w, tok, acc, kbuf, vbuf, qbuf, meta, own, rx, ry, mem, stage,
+    wst, w, tok, acc, kbuf, vbuf, qbuf, meta, own, rx, ry, mem, stage,
     recv, send, csem_l, csem_s, csem_r, dsem_s, dsem_r, osem_l, osem_s, osem_r,
 ):
     seg = lax.axis_index("seg")
@@ -63,31 +58,30 @@
     sibling = device(x, y, 1 - c, z)
 
     barrier = pltpu.get_barrier_semaphore()
-    peers = [sibling, shifted("z", 1), shifted("z", -1)]
-    for dim in "xy":
+    peers = [sibling]
+    for dim in "xyz":
         peers += [shifted(dim, k) for k in range(1, dims[dim])]
     for peer in peers:
         pl.semaphore_signal(barrier, inc=1, device_id=peer, device_id_type=MESH_ID)
     pl.semaphore_wait(barrier, len(peers))
 
+    def columns(core):
+        wide = pl.ds(pl.multiple_of(core * CW, CW), CW)
+        return (wk_hbm.at[:, wide], wv_hbm.at[:, wide], wq_hbm.at[:, pl.ds(pl.multiple_of(core * 4 * CW, CW), 4 * CW)])
+
+    spans = (slice(0, CW), slice(CW, 2 * CW), slice(2 * CW, 6 * CW))
     locals_, sends_, recvs_ = [], [], []
-
-    def columns(ch, core):
-        if ch < 2:
-            return (wk_hbm, wv_hbm)[ch].at[:, pl.ds(pl.multiple_of(core * CW, CW), CW)]
-        return wq_hbm.at[:, pl.ds(pl.multiple_of(core * 4 * CW + (ch - 2) * CW, CW), CW)]
-
-    for ch in range(NCH):
-        slot = w.at[ch, y, x, c, z]
-        other = w.at[ch, y, x, 1 - c, z]
+    for i, span in enumerate(spans):
         there = pltpu.make_async_remote_copy(
-            columns(ch, 1 - c), slot, csem_s.at[ch], csem_r.at[ch], device_id=sibling, device_id_type=MESH_ID
+            columns(1 - c)[i], wst.at[c, :, span], csem_s.at[i], csem_r.at[i],
+            device_id=sibling, device_id_type=MESH_ID,
         )
         there.start()
-        here = pltpu.make_async_copy(columns(ch, c), slot, csem_l.at[ch])
+        here = pltpu.make_async_copy(columns(c)[i], wst.at[c, :, span], csem_l.at[i])
         here.start()
+        other = wst.at[1 - c, :, span]
         back = pltpu.make_async_remote_copy(
-            other, other, csem_s.at[ch], csem_r.at[ch], device_id=sibling, device_id_type=MESH_ID
+            other, other, csem_s.at[i], csem_r.at[i], device_id=sibling, device_id_type=MESH_ID
         )
         locals_.append(here)
         sends_.append(there)
@@ -96,78 +90,76 @@
     row8 = lax.broadcasted_iota(jnp.int32, (8, HEAD), 0)
     meta[c] = jnp.where(row8 == 0, valid_ref[0, 0], mask_ref[1, 0])
     meta_copy = pltpu.make_async_remote_copy(
-        meta.at[c], meta.at[c], csem_s.at[NCH], csem_r.at[NCH], device_id=sibling, device_id_type=MESH_ID
+        meta.at[c], meta.at[c], csem_s.at[3], csem_r.at[3], device_id=sibling, device_id_type=MESH_ID
     )
     meta_back = pltpu.make_async_remote_copy(
-        meta.at[1 - c], meta.at[1 - c], csem_s.at[NCH], csem_r.at[NCH], device_id=sibling, device_id_type=MESH_ID
+        meta.at[1 - c], meta.at[1 - c], csem_s.at[3], csem_r.at[3], device_id=sibling, device_id_type=MESH_ID
     )
     tok_copy = pltpu.make_async_remote_copy(
-        tok_hbm, tok.at[c], csem_s.at[NCH + 1], csem_r.at[NCH + 1], device_id=sibling, device_id_type=MESH_ID
+        tok_hbm, tok.at[c], csem_s.at[4], csem_r.at[4], device_id=sibling, device_id_type=MESH_ID
     )
     tok_back = pltpu.make_async_remote_copy(
-        tok.at[1 - c], tok.at[1 - c], csem_s.at[NCH + 1], csem_r.at[NCH + 1], device_id=sibling, device_id_type=MESH_ID
-    )
-    tok_here = pltpu.make_async_copy(tok_hbm, tok.at[c], csem_l.at[NCH])
-
-    def block(ch, order, stage_no, index, half):
-        cols = slice(None) if half is None else pl.ds(half * (CW // 2), CW // 2)
+        tok.at[1 - c], tok.at[1 - c], csem_s.at[4], csem_r.at[4], device_id=sibling, device_id_type=MESH_ID
+    )
+    tok_here = pltpu.make_async_copy(tok_hbm, tok.at[c], csem_l.at[3])
+
+    def block(ch, stage_no, index):
+        order = ORDERS[ch % 6]
         at = {d: pl.ds(pos[d], 1) for d in "xyz"}
         for d in order[:stage_no]:
             at[d] = slice(None)
         at[order[stage_no]] = pl.ds(index, 1)
-        return w.at[ch, at["y"], at["x"], :, at["z"], :, cols]
+        return w.at[ch, at["y"], at["x"], :, at["z"]]
 
     steps = {}
     for ch in range(NCH):
-        order = ORDERS[ch % 3]
-        steps[ch] = [(s, k) for s in range(3) for k in range(1, dims[order[s]] // 2 + 1)]
-
-    def ring(ch, number, arriving):
-        order = ORDERS[ch % 3]
-        s, k = steps[ch][number]
-        dim = order[s]
-        n = dims[dim]
-        copies = []
-        for side, delta in ((0, 1), (1, -1)):
-            back = k if arriving else k - 1
-            index = lax.rem(pos[dim] - delta * back + n, n)
-            half = side if 2 * k == n else None
-            piece = block(ch, order, s, index, half)
-            copies.append(
+        steps[ch] = []
+        for s, kind in enumerate(KINDS):
+            n = dims[ORDERS[ch % 6][s]]
+            if kind == DIRECT:
+                steps[ch].append([(s, k, 0, -k) for k in range(1, n)])
+                continue
+            for k in range(1, n // 2 + 1):
+                sides = (1, -1) if 2 * k < n else ((1,) if ch // 3 % 2 == 0 else (-1,))
+                steps[ch].append([(s, side, -side * (k - 1), -side * k) for side in sides])
+
+    def copies(ch, number, arriving):
+        first = sum(len(step) for step in steps[ch][:number])
+        made = []
+        for m, (s, hop, sent_off, arrive_off) in enumerate(steps[ch][number]):
+            dim = ORDERS[ch % 6][s]
+            n = dims[dim]
+            index = lax.rem(pos[dim] + (arrive_off if arriving else sent_off) + n, n)
+            piece = block(ch, s, index)
+            made.append(
                 pltpu.make_async_remote_copy(
-                    piece, piece, send.at[ch, number, side], recv.at[ch, number, side],
-                    device_id=shifted(dim, delta), device_id_type=MESH_ID,
+                    piece, piece, send.at[ch, first + m], recv.at[ch, first + m],
+                    device_id=shifted(dim, hop), device_id_type=MESH_ID,
                 )
             )
-        return copies
+        return made
 
     sent = []
 
     def tick(ch, number):
-        arrived = ring(ch, number - 1, True) if number else None
-        leaving = ring(ch, number, False) if number < len(steps[ch]) else None
-        if number == 0:
-            locals_[ch].wait()
-            recvs_[ch].wait_recv()
-        same_stage = leaving is not None and number and steps[ch][number][0] == steps[ch][number - 1][0]
-        if same_stage:
-            for a, b in zip(arrived, leaving):
-                a.wait_recv()
-                b.start()
+        arrived = copies(ch, number - 1, True) if number else []
+        leaving = copies(ch, number, False) if number < len(steps[ch]) else []
+        paired = number and number < len(steps[ch]) and steps[ch][number][0][0] == steps[ch][number - 1][0][0]
+        if paired and len(arrived) == len(leaving):
+            for one, two in zip(arrived, leaving):
+                one.wait_recv()
+                two.start()
         else:
-            if arrived is not None:
-                for a in arrived:
-                    a.wait_recv()
-            if leaving is not None:
-                for b in leaving:
-                    b.start()
-        if leaving is not None:
-            sent.extend(leaving)
+            for one in arrived:
+                one.wait_recv()
+            for two in leaving:
+                two.start()
+        sent.extend(leaving)
 
     def project(ch, dst):
         def part(i, first):
+            b = jnp.concatenate([w[ch, i].reshape(1024, HEAD), w[ch + 1, i].reshape(1024, HEAD)], axis=1)
             a = tok[:, :, pl.ds(pl.multiple_of(i * 1024, 1024), 1024)].reshape(2 * SEG, 1024)
-            b = w[ch, i].reshape(1024, CW)
             r = jnp.dot(a, b, preferred_element_type=F32)
             if first:
                 acc[...] = r
@@ -294,13 +286,18 @@
         finals.append((there, here))
 
     finals = []
+    for here, back in zip(locals_, recvs_):
+        here.wait()
+        back.wait_recv()
+    for ch in range(NCH):
+        w[ch, y, x, :, z] = wst[:, :, ch * HEAD : (ch + 1) * HEAD]
     for item in PROGRAM:
         if item == "keys":
             tok_here.wait()
             tok_back.wait_recv()
             project(0, kbuf)
         elif item == "values":
-            project(1, vbuf)
+            project(2, vbuf)
         elif item == "delta":
             meta_back.wait_recv()
             delta()
@@ -310,12 +307,12 @@
         elif item == "memory":
             memory()
         elif item[0] == "q":
-            project(2 + int(item[1]), qbuf.at[int(item[1])])
+            project(4 + 2 * int(item[1]), qbuf.at[int(item[1])])
         elif item[0] == "a":
             attend(int(item[1]))
         else:
             tick(*item)
-            if item == (2, 0):
+            if item == (NCH - 1, 0):
                 meta_copy.start()
                 tok_copy.start()
                 tok_here.start()
@@ -347,7 +344,8 @@
             in_specs=[hbm] * 4 + [smem] * 3,
             out_specs=hbm,
             scratch_shapes=[
-                pltpu.VMEM((NCH, y, x, 2, nz, 16, CW), BF16),
+                pltpu.VMEM((2, 16, NCH * HEAD), BF16),
+                pltpu.VMEM((NCH, y, x, 2, nz, 16, HEAD), BF16),
                 pltpu.VMEM((2, SEG, 4096), BF16),
                 pltpu.VMEM((2 * SEG, CW), F32),
                 pltpu.VMEM((2, SEG, CW), BF16),
@@ -359,11 +357,11 @@
                 pltpu.VMEM((y, 2, HEAD + 16, HEAD), BF16),
                 pltpu.VMEM((2, 2, HEAD, 2 * HEAD), BF16),
                 pltpu.VMEM((4, 2, SEG, CW), BF16),
-                dma((NCH, 8, 2)),
-                dma((NCH, 8, 2)),
-                dma((NCH + 1,)),
-                dma((NCH + 2,)),
-                dma((NCH + 2,)),
+                dma((NCH, x + y + nz - 3)),
+                dma((NCH, x + y + nz - 3)),
+                dma((4,)),
+                dma((5,)),
+                dma((5,)),
                 dma((2, 3)),
                 dma((2, 3)),
                 dma((4,)),

time: 104 us -> 89.3 us (0.86)
  Pallas kernels: 101 us -> 86.1 us
    pallas_call x1, Pallas kernels: 101 us -> 86.1 us  [shards(): pl.pallas_call(functools.partial(body, dims), out_shape=jax.ShapeDtypeStr...]
where the time goes in v2:
time: 89.3 us; the launch traced here: 89.1 us
  Pallas kernels  86.1 us (96%)
  local copies, waits for them, and re-layouts  2.3 us (3%)
    pallas_call x1, Pallas kernels, shards(): pl.pallas_call(functools.partial(body, dims), out_shape=jax.ShapeDtypeStr...  86.1 us
    unnamed x1, local copies, waits for them, and re-layouts  2.3 us

profile of v2, /device:TPU:1, one launch (start us, length us, event | category | flops | bytes accessed | tf_op | source)
XLA Modules:
  0.0 89.1 jit_solution(6270985882189163731)
XLA Ops:
  0.7 86.1 %shard_map.73 = bf16[256,2048]{1,0:T(8,128)(2,1)} custom-call(bf16[256,4096]{1,0:T(8,128)(2,1)} %bitcast.4, bf16[16,2048]{1,0:T(8,128)(2,1)} %wq_hbm.1, bf16[16,512]{1,0:T(8,128)(2,1)} %wk_hbm.1, bf16[16,512]{1,0:T(8,128)(2,1)} %wv_hbm.1, f32[16]{0:T(128)} %gate_ref.1, s32[2,2]{1,0:T(2,128)} %bitcast.5, s32[1,1]{1,0:T(1,128)S(6)} %copy.9.valid_ref), custom_call_target="tpu_custom_call" | custom-call | tf_op jit(solution)/shard_map/pallas_call | solution.py:341
  86.8 2.3 %copy.10 = bf16[1,256,2048]{2,1,0:T(8,128)(2,1)} copy(bf16[1,256,2048]{2,1,0:T(8,128)(2,1)} %bitcast.3) | data formatting | bytes 2097152

commit v3 on v2

v3 whole, which is shorter than its diff:
```python
import functools

import jax
import jax.numpy as jnp
from jax import lax
from jax.experimental import pallas as pl
from jax.experimental.pallas import tpu as pltpu
from jax.sharding import PartitionSpec as P

HEAD = 128
SEG = 256
CW = 256
NCH = 12
DIRECT, TWO, RING = "direct", "two", "ring"
ORDERS = ("zyx", "zxy", "zyx", "yxz", "zxy", "xyz", "xzy", "zyx", "xyz", "zxy", "yzx", "yxz")
KINDS = (
    (DIRECT, DIRECT, 2, 0), (DIRECT, DIRECT, 2, 0), (DIRECT, RING, 2, 0),
    (DIRECT, DIRECT, 2, 1), (DIRECT, RING, 2, 0), (DIRECT, RING, 2, 0),
    (DIRECT, RING, 2, 1), (TWO, RING, 2, 1), (DIRECT, DIRECT, 2, 0),
    (TWO, RING, 2, 1), (DIRECT, RING, 2, 1), (DIRECT, DIRECT, 2, 1),
)
MESH_ID = pl.DeviceIdType.MESH
F32 = jnp.float32
LOG2E = 1.4426950408889634
BF16 = jnp.bfloat16

PROGRAM = (
    (5, None, 0), (0, None, 0), (1, None, 0), (2, None, 0), (3, None, 0), (10, None, 0), (6, None, 0), (4, None, 0),
    (7, None, 0), (9, None, 0), (5, None, 1), (3, None, 1), (6, None, 1), (0, None, 1), (10, None, 1), (8, None, 0),
    (1, None, 1), (5, None, 2), (2, None, 1), (3, None, 2), (3, 0, 0), (3, 1, 0), (8, None, 1), (4, None, 1),
    (7, None, 1), (9, None, 1), (0, None, 2), (0, 0, 0), (0, 1, 0), (6, None, 2), (5, None, 3), (5, 0, 0),
    (5, 1, 0), (10, None, 2), (1, None, 2), (1, 0, 0), (1, 1, 0), (2, None, 2), (3, 0, 1), (4, None, 2),
    (8, None, 2), (3, 1, 1), (7, None, 2), (9, None, 2), (6, None, 3), (0, 0, 1), (1, 0, 1), (5, 0, 1),
    (11, None, 0), (5, 1, 1), (0, 1, 1), (10, None, 3), (1, 1, 1), (4, None, 3), (4, 0, 0), (4, 1, 0), (3, 0, 2),
    (2, None, 3), (2, 0, 0), (2, 1, 0), (9, None, 3), (3, 1, 2), (7, None, 3), (6, None, 4), (0, 1, 2), (5, 0, 2),
    (0, 0, 2), (1, 1, 2), (1, 0, 2), ("keys", 0), (5, 1, 2), ("keys", 1), (11, None, 1), ("keys", 2), (10, None, 4),
    ("keys", 3), (2, 0, 1), (3, 0, 3), (8, 0, 0), (4, 0, 1), (3, 1, 3), (8, 1, 0), (6, None, 5), (6, 0, 0),
    (2, 1, 1), (9, None, 4), (5, 0, 3), (4, 1, 1), (6, 1, 0), (7, None, 4), (7, 0, 0), (7, 1, 0), (11, None, 2),
    (11, 0, 0), (3, 0, 4), (5, 1, 3), (11, 1, 0), (10, None, 5), (2, 0, 2), (4, 0, 2), (8, 0, 1), (2, 1, 2),
    (3, 1, 4), ("values", 0), ("values", 1), ("values", 2), (5, 0, 4), ("values", 3), (6, 0, 1), (9, 0, 0),
    ("delta",), (8, 1, 1), (4, 1, 2), (7, 0, 1), (10, 0, 0), (11, 0, 1), (5, 1, 4), ("q", 0, 0), ("q", 0, 1),
    (6, 1, 1), (9, 1, 0), (7, 1, 1), (10, 1, 0), ("q", 0, 2), ("q", 0, 3), (11, 1, 1), ("local", 0, 0),
    ("local", 0, 1), (6, 0, 2), (8, 0, 2), ("rows",), (8, 1, 2), (9, 0, 1), (11, 0, 2), (6, 1, 2), (7, 0, 2),
    (11, 1, 2), (8, 0, 3), (9, 1, 1), (10, 0, 1), (7, 1, 2), ("q", 1, 0), ("q", 1, 1), (8, 1, 3), ("q", 1, 2),
    ("q", 1, 3), ("local", 1, 0), ("local", 1, 1), (11, 0, 3), (10, 1, 1), ("memory",), (8, 0, 4), (11, 1, 3),
    ("finish", 0, 0), ("finish", 0, 1), ("finish", 1, 0), ("finish", 1, 1), (9, 0, 2), (8, 1, 4), (10, 0, 2),
    (9, 1, 2), ("q", 2, 0), ("q", 2, 1), ("q", 2, 2), (11, 0, 4), ("q", 2, 3), ("local", 2, 0), (11, 1, 4),
    ("finish", 2, 0), ("local", 2, 1), ("finish", 2, 1), (10, 1, 2), ("q", 3, 0), ("q", 3, 1), ("q", 3, 2),
    ("q", 3, 3), ("local", 3, 0), ("finish", 3, 0), ("local", 3, 1), ("finish", 3, 1),
)


def sigma(v):
    return jnp.where(v > 0, v, jnp.exp(jnp.minimum(v, 0.0)) - 1.0) + 1.0


def body(
    dims,
    tok_hbm, wq_hbm, wk_hbm, wv_hbm, gate_ref, mask_ref, valid_ref,
    out_ref,
    wst, w, tok, acc, kbuf, vbuf, qbuf, meta, own, rx, ry, mem, loc, stage,
    recv, send, csem_l, csem_s, csem_r, dsem_s, dsem_r, osem_s, osem_r,
):
    seg = lax.axis_index("seg")
    z = lax.axis_index("fsdp")
    c = lax.rem(seg, 2)
    x = lax.rem(seg // 2, dims["x"])
    y = seg // (2 * dims["x"])
    pos = {"x": x, "y": y, "z": z}

    def device(xx, yy, cc, zz):
        return {"seg": (yy * dims["x"] + xx) * 2 + cc, "fsdp": zz}

    def shifted(dim, delta):
        at = dict(pos)
        at[dim] = lax.rem(pos[dim] + delta + dims[dim], dims[dim])
        return device(at["x"], at["y"], c, at["z"])

    sibling = device(x, y, 1 - c, z)

    barrier = pltpu.get_barrier_semaphore()
    peers = [sibling]
    for dim in "xyz":
        peers += [shifted(dim, k) for k in range(1, dims[dim])]
    for peer in peers:
        pl.semaphore_signal(barrier, inc=1, device_id=peer, device_id_type=MESH_ID)
    pl.semaphore_wait(barrier, len(peers))

    def columns(core):
        wide = pl.ds(pl.multiple_of(core * CW, CW), CW)
        return (wk_hbm.at[:, wide], wv_hbm.at[:, wide], wq_hbm.at[:, pl.ds(pl.multiple_of(core * 4 * CW, CW), 4 * CW)])

    spans = (slice(0, CW), slice(CW, 2 * CW), slice(2 * CW, 6 * CW))
    locals_, sends_, recvs_ = [], [], []
    for i, span in enumerate(spans):
        there = pltpu.make_async_remote_copy(
            columns(1 - c)[i], wst.at[c, :, span], csem_s.at[i], csem_r.at[i],
            device_id=sibling, device_id_type=MESH_ID,
        )
        there.start()
        here = pltpu.make_async_copy(columns(c)[i], wst.at[c, :, span], csem_l.at[i])
        here.start()
        other = wst.at[1 - c, :, span]
        back = pltpu.make_async_remote_copy(
            other, other, csem_s.at[i], csem_r.at[i], device_id=sibling, device_id_type=MESH_ID
        )
        locals_.append(here)
        sends_.append(there)
        recvs_.append(back)

    row8 = lax.broadcasted_iota(jnp.int32, (8, HEAD), 0)
    meta[c] = jnp.where(row8 == 0, valid_ref[0, 0], mask_ref[1, 0])
    meta_copy = pltpu.make_async_remote_copy(
        meta.at[c], meta.at[c], csem_s.at[3], csem_r.at[3], device_id=sibling, device_id_type=MESH_ID
    )
    meta_back = pltpu.make_async_remote_copy(
        meta.at[1 - c], meta.at[1 - c], csem_s.at[3], csem_r.at[3], device_id=sibling, device_id_type=MESH_ID
    )
    tok_copy = pltpu.make_async_remote_copy(
        tok_hbm, tok.at[c], csem_s.at[4], csem_r.at[4], device_id=sibling, device_id_type=MESH_ID
    )
    tok_back = pltpu.make_async_remote_copy(
        tok.at[1 - c], tok.at[1 - c], csem_s.at[4], csem_r.at[4], device_id=sibling, device_id_type=MESH_ID
    )
    tok_here = pltpu.make_async_copy(tok_hbm, tok.at[c], csem_l.at[3])

    def block(ch, stage_no, index, sub):
        order = ORDERS[ch]
        at = {d: pl.ds(pos[d], 1) for d in "xyz"}
        for d in order[:stage_no]:
            at[d] = slice(None)
        at[order[stage_no]] = pl.ds(index, 1)
        cores = slice(None) if sub is None else pl.ds(sub, 1)
        return w.at[ch, at["y"], at["x"], cores, at["z"]]

    def stage_steps(ch, s, kind, even):
        n = dims[ORDERS[ch][s]]
        if kind == DIRECT:
            return [[(s, k, 0, -k) for k in range(1, n)]]
        if kind == TWO and n == 8:
            far = (s, 2, -2, -4) if even else (s, -2, 2, 4)
            return [
                [(s, 1, 0, -1), (s, -1, 0, 1), (s, 2, 0, -2), (s, -2, 0, 2)],
                [(s, -1, 2, 3), (s, 1, -2, -3), far],
            ]
        made = []
        for k in range(1, n // 2 + 1):
            sides = (1, -1) if 2 * k < n else ((1,) if even else (-1,))
            made.append([(s, side, -side * (k - 1), -side * k) for side in sides])
        return made

    threads = {}
    for ch in range(NCH):
        k1, k2, subs, odd = KINDS[ch]
        even = not odd
        steps = stage_steps(ch, 0, k1, even) + stage_steps(ch, 1, k2, even)
        threads[ch, None] = (steps, None, 0)
        used = sum(len(step) for step in steps)
        for h in range(subs):
            steps = stage_steps(ch, 2, RING, h == 0 if subs == 2 else even)
            threads[ch, h] = (steps, h if subs == 2 else None, used)
            used += sum(len(step) for step in steps)

    def copies(thread, number, arriving):
        ch = thread[0]
        steps, sub, first = threads[thread]
        first += sum(len(step) for step in steps[:number])
        made = []
        for m, (s, hop, sent_off, arrive_off) in enumerate(steps[number]):
            dim = ORDERS[ch][s]
            n = dims[dim]
            index = lax.rem(pos[dim] + (arrive_off if arriving else sent_off) + n, n)
            piece = block(ch, s, index, sub)
            made.append(
                pltpu.make_async_remote_copy(
                    piece, piece, send.at[ch, first + m], recv.at[ch, first + m],
                    device_id=shifted(dim, hop), device_id_type=MESH_ID,
                )
            )
        return made

    sent = []

    def tick(ch, sub, number):
        thread = (ch, sub)
        steps = threads[thread][0]
        arrived = copies(thread, number - 1, True) if number else []
        leaving = copies(thread, number, False) if number < len(steps) else []
        paired = arrived and leaving and steps[number][0][0] == steps[number - 1][0][0]
        if paired and TWO not in KINDS[ch] and len(arrived) == len(leaving):
            for one, two in zip(arrived, leaving):
                one.wait_recv()
                two.start()
        else:
            for one in arrived:
                one.wait_recv()
            for two in leaving:
                two.start()
        sent.extend(leaving)

    def project(pair, i, dst):
        ch = 2 * pair
        b = jnp.concatenate([w[ch, i].reshape(1024, HEAD), w[ch + 1, i].reshape(1024, HEAD)], axis=1)
        a = tok[:, :, i * 1024 : (i + 1) * 1024].reshape(2 * SEG, 1024)
        r = jnp.dot(a, b, preferred_element_type=F32)
        if i:
            r += acc[pair]
        if i < 3:
            acc[pair] = r
        else:
            dst[...] = r.astype(BF16).reshape(2, SEG, CW)

    def delta():
        jrow = lax.broadcasted_iota(jnp.int32, (SEG, HEAD), 0)
        for g in range(2):
            cols = slice(g * HEAD, (g + 1) * HEAD)
            both = []
            for s in range(2):
                live = jrow < meta[s, 0:1, :]
                sig = jnp.where(live, sigma(kbuf[s, :, cols].astype(F32)), 0.0)
                zrow = jnp.sum(sig, axis=0, keepdims=True)
                m = lax.dot_general(
                    sig.astype(BF16), vbuf[s, :, cols], (((0,), (0,)), ((), ())), preferred_element_type=F32
                )
                both.append((m, zrow))
            own[g, 0:HEAD, :] = both[0][0]
            own[g, HEAD : HEAD + 16, :] = jnp.broadcast_to(both[0][1], (16, HEAD))
            rx[x, g, 0:HEAD, :] = (both[0][0] + both[1][0]).astype(BF16)
            rx[x, g, HEAD : HEAD + 16, :] = jnp.broadcast_to(both[0][1] + both[1][1], (16, HEAD)).astype(BF16)

    def exchange(dim, buf, number, arriving):
        n = dims[dim]
        copies = []
        for k in range(1, n):
            index = lax.rem(pos[dim] - k + n, n) if arriving else pos[dim]
            copies.append(
                pltpu.make_async_remote_copy(
                    buf.at[index], buf.at[index], dsem_s.at[number, k - 1], dsem_r.at[number, k - 1],
                    device_id=shifted(dim, k), device_id_type=MESH_ID,
                )
            )
        return copies

    def launch(copies):
        for one in copies:
            one.start()
        sent.extend(copies)

    def row_totals():
        for one in exchange("x", rx, 0, True):
            one.wait_recv()
        for g in range(2):
            total = jnp.zeros((HEAD + 16, HEAD), F32)
            for k in range(dims["x"]):
                total = total + rx[k, g].astype(F32)
            ry[y, g] = total.astype(BF16)
        launch(exchange("y", ry, 1, False))

    def memory():
        for one in exchange("y", ry, 1, True):
            one.wait_recv()
        for g in range(2):
            total = jnp.zeros((HEAD + 16, HEAD), F32)
            for k in range(dims["x"]):
                total = total + jnp.where(k < x, rx[k, g].astype(F32), 0.0)
            for k in range(dims["y"]):
                total = total + jnp.where(k < y, ry[k, g].astype(F32), 0.0)
            for s in range(2):
                if s:
                    total = total + own[g]
                mem[s, g, :, 0:HEAD] = total[0:HEAD].astype(BF16)
                zcol = jnp.transpose(jnp.broadcast_to(total[HEAD : HEAD + 1], (HEAD, HEAD)))
                mem[s, g, :, HEAD:] = zcol.astype(BF16)

    ones = jnp.ones((SEG, HEAD), BF16)

    def sides(j):
        return [jax.nn.sigmoid(jnp.full((1, HEAD), gate_ref[c * 8 + 2 * j + e], F32)) for e in range(2)]

    def stacked(j, s, rows):
        return jnp.concatenate([qbuf[j, s, rows, 0:HEAD], qbuf[j, s, rows, HEAD:]], axis=0)

    def attend(j, second):
        s = c if second else 1 - c
        kcols = slice(j // 2 * HEAD, (j // 2 + 1) * HEAD)
        gates = sides(j)
        valid = meta[s, 0:1, :]
        for r in range(2):
            nk = (r + 1) * HEAD
            rows = slice(r * HEAD, (r + 1) * HEAD)
            keys = kbuf[s, 0:nk, kcols]
            vals = jnp.concatenate([vbuf[s, 0:nk, kcols], ones[0:nk]], axis=1)
            scores = lax.dot_general(
                stacked(j, s, rows), keys, (((1,), (1,)), ((), ())), preferred_element_type=F32
            )
            irow = lax.broadcasted_iota(jnp.int32, (HEAD, nk), 0) + r * HEAD
            jcol = lax.broadcasted_iota(jnp.int32, (HEAD, nk), 1)
            wide = valid if r == 0 else jnp.concatenate([valid, valid], axis=1)
            allowed = (jcol <= irow) & (jcol < wide)
            if r:
                lower = jnp.concatenate([meta[s, 1:2, :], jnp.ones((1, HEAD), jnp.int32)], axis=1)
                allowed = allowed & (lower > 0)
            allowed = jnp.concatenate([allowed, allowed], axis=0)
            masked = jnp.where(allowed, scores, -1e30)
            top = jnp.max(masked, axis=1, keepdims=True)
            expo = jnp.exp2((masked - top) * (HEAD**-0.5 * LOG2E)).astype(BF16)
            local = jnp.dot(expo, vals, preferred_element_type=F32)
            local = local[:, 0:HEAD] / jnp.maximum(local[:, HEAD:], 1.0)
            for e in range(2):
                half = slice(e * HEAD, (e + 1) * HEAD)
                loc[j, s, rows, half] = (1.0 - gates[e]) * local[half]

    def finish(j, second):
        s = c if second else 1 - c
        gates = sides(j)
        valid = meta[s, 0:1, :]
        first = pl.multiple_of(c * 4 * CW + j * CW, CW)
        for r in range(2):
            rows = slice(r * HEAD, (r + 1) * HEAD)
            sq = sigma(stacked(j, s, rows).astype(F32)).astype(BF16)
            retrieved = jnp.dot(sq, mem[s, j // 2], preferred_element_type=F32)
            remembered = retrieved[:, 0:HEAD] / (retrieved[:, HEAD:] + 1.0)
            alive = (lax.broadcasted_iota(jnp.int32, (HEAD, HEAD), 0) + r * HEAD) < valid
            for e in range(2):
                half = slice(e * HEAD, (e + 1) * HEAD)
                mixed = gates[e] * remembered[half] + loc[j, s, rows, half]
                mixed = jnp.where(alive, mixed, 0.0).astype(BF16)
                if second:
                    out_ref[rows, pl.ds(first + e * HEAD, HEAD)] = mixed
                else:
                    stage[j, rows, half] = mixed
        if not second:
            one = pltpu.make_async_remote_copy(
                stage.at[j], out_ref.at[:, pl.ds(first, CW)], osem_s.at[j], osem_r.at[j],
                device_id=sibling, device_id_type=MESH_ID,
            )
            one.start()
            sent.append(one)

    for here, back in zip(locals_, recvs_):
        here.wait()
        back.wait_recv()
    for ch in range(NCH):
        w[ch, y, x, :, z] = wst[:, :, ch * HEAD : (ch + 1) * HEAD]
    meta_copy.start()
    tok_copy.start()
    tok_here.start()
    for name, *where in PROGRAM:
        if name == "keys":
            if where[0] == 0:
                tok_here.wait()
                tok_back.wait_recv()
            project(0, where[0], kbuf)
        elif name == "values":
            project(1, where[0], vbuf)
        elif name == "q":
            project(2 + where[0], where[1], qbuf.at[where[0]])
        elif name == "delta":
            meta_back.wait_recv()
            delta()
            launch(exchange("x", rx, 0, False))
        elif name == "rows":
            row_totals()
        elif name == "memory":
            memory()
        elif name == "local":
            attend(where[0], where[1])
        elif name == "finish":
            finish(where[0], where[1])
        else:
            tick(name, *where)

    for j in range(4):
        arriving = out_ref.at[:, pl.ds(pl.multiple_of((1 - c) * 4 * CW + j * CW, CW), CW)]
        pltpu.make_async_remote_copy(
            stage.at[j], arriving, osem_s.at[j], osem_r.at[j], device_id=sibling, device_id_type=MESH_ID
        ).wait_recv()
    for one in sent + sends_ + [meta_copy, tok_copy]:
        one.wait_send()


def solution(mesh):
    segs, nz = mesh.shape["seg"], mesh.shape["fsdp"]
    side = {32: 4, 8: 2, 16: 4}[segs]
    dims = {"x": side, "y": segs // 2 // side, "z": nz}

    def shards(tokens, w_query, w_key, value_weight, gate_bias, block_mask, valid_len):
        hbm = pl.BlockSpec(memory_space=pltpu.HBM)
        smem = pl.BlockSpec(memory_space=pltpu.SMEM)
        x, y, nz = dims["x"], dims["y"], dims["z"]
        dma = pltpu.SemaphoreType.DMA
        out = pl.pallas_call(
            functools.partial(body, dims),
            out_shape=pltpu.VMEM((SEG, 2048), BF16),
            in_specs=[hbm] * 4 + [smem] * 3,
            out_specs=pl.BlockSpec(memory_space=pltpu.VMEM),
            scratch_shapes=[
                pltpu.VMEM((2, 16, NCH * HEAD), BF16),
                pltpu.VMEM((NCH, y, x, 2, nz, 16, HEAD), BF16),
                pltpu.VMEM((2, SEG, 4096), BF16),
                pltpu.VMEM((6, 2 * SEG, CW), F32),
                pltpu.VMEM((2, SEG, CW), BF16),
                pltpu.VMEM((2, SEG, CW), BF16),
                pltpu.VMEM((4, 2, SEG, CW), BF16),
                pltpu.VMEM((2, 8, HEAD), jnp.int32),
                pltpu.VMEM((2, HEAD + 16, HEAD), F32),
                pltpu.VMEM((x, 2, HEAD + 16, HEAD), BF16),
                pltpu.VMEM((y, 2, HEAD + 16, HEAD), BF16),
                pltpu.VMEM((2, 2, HEAD, 2 * HEAD), BF16),
                pltpu.VMEM((4, 2, SEG, CW), F32),
                pltpu.VMEM((4, SEG, CW), BF16),
                dma((NCH, 20)),
                dma((NCH, 20)),
                dma((4,)),
                dma((5,)),
                dma((5,)),
                dma((2, 3)),
                dma((2, 3)),
                dma((4,)),
                dma((4,)),
            ],
            compiler_params=pltpu.CompilerParams(
                collective_id=0, has_side_effects=True, vmem_limit_bytes=56 * 1024 * 1024
            ),
        )(tokens[0], w_query, w_key, value_weight, gate_bias, block_mask[0, 0], valid_len)
        return out[None]

    in_specs = (
        P("fsdp", "seg", None),
        P(("seg", "fsdp"), None),
        P(("seg", "fsdp"), None),
        P(("seg", "fsdp"), None),
        P(),
        P("fsdp", "seg", None, None),
        P("fsdp", "seg"),
    )
    return jax.shard_map(
        shards, mesh=mesh, in_specs=in_specs, out_specs=P("fsdp", "seg", None), check_vma=False
    )
```

time: 89.3 us -> 83.5 us (0.935)
  Pallas kernels: 86.1 us -> 81.7 us
  local copies, waits for them, and re-layouts: 2.3 us -> 0.97 us
    pallas_call x1, Pallas kernels: 86.1 us -> 81.7 us  [shards(): pl.pallas_call(functools.partial(body, dims), out_shape=pltpu.VMEM((SEG,...]
    unnamed x1, local copies, waits for them, and re-layouts: 2.3 us -> 0.97 us
where the time goes in v3:
time: 83.5 us; the launch traced here: 83.3 us
  Pallas kernels  81.7 us (98%)
  local copies, waits for them, and re-layouts  0.97 us (1%)
    pallas_call x1, Pallas kernels, shards(): pl.pallas_call(functools.partial(body, dims), out_shape=pltpu.VMEM((SEG,...  81.7 us

profile of v3, /device:TPU:1, one launch (start us, length us, event | category | flops | bytes accessed | tf_op | source)
XLA Modules:
  0.0 83.3 jit_solution(7320300090850660852)
XLA Ops:
  0.7 81.7 %shard_map.73 = bf16[256,2048]{1,0:T(8,128)(2,1)S(1)} custom-call(bf16[256,4096]{1,0:T(8,128)(2,1)} %bitcast.4, bf16[16,2048]{1,0:T(8,128)(2,1)} %wq_hbm.1, bf16[16,512]{1,0:T(8,128)(2,1)} %wk_hbm.1, bf16[16,512]{1,0:T(8,128)(2,1)} %wv_hbm.1, f32[16]{0:T(128)} %gate_ref.1, s32[2,2]{1,0:T(2,128)} %bitcast.5, s32[1,1]{1,0:T(1,128)S(6)} %copy.10.valid_ref), custom_call_target="tpu_custom_call" | custom-call | tf_op jit(solution)/shard_map/pallas_call | solution.py:392
  82.4 1.0 %copy.9 = bf16[1,256,2048]{2,1,0:T(8,128)(2,1)} copy(bf16[1,256,2048]{2,1,0:T(8,128)(2,1)S(1)} %bitcast.3) | data formatting | bytes 2097152

commit v4 on v3

--- a/solution.py
+++ b/solution.py
@@ -12,12 +12,12 @@
 CW = 256
 NCH = 12
 DIRECT, TWO, RING = "direct", "two", "ring"
-ORDERS = ("zyx", "zxy", "zyx", "yxz", "zxy", "xyz", "xzy", "zyx", "xyz", "zxy", "yzx", "yxz")
+ORDERS = ("zyx", "zxy", "xyz", "xyz", "zyx", "zxy", "yxz", "xyz", "zyx", "zyx", "zxy", "zxy")
 KINDS = (
-    (DIRECT, DIRECT, 2, 0), (DIRECT, DIRECT, 2, 0), (DIRECT, RING, 2, 0),
-    (DIRECT, DIRECT, 2, 1), (DIRECT, RING, 2, 0), (DIRECT, RING, 2, 0),
-    (DIRECT, RING, 2, 1), (TWO, RING, 2, 1), (DIRECT, DIRECT, 2, 0),
-    (TWO, RING, 2, 1), (DIRECT, RING, 2, 1), (DIRECT, DIRECT, 2, 1),
+    (DIRECT, DIRECT, 2, 0), (DIRECT, DIRECT, 2, 0), (DIRECT, DIRECT, 1, 1),
+    (DIRECT, RING, 1, 0), (TWO, RING, 2, 1), (TWO, RING, 2, 1),
+    (DIRECT, RING, 1, 0), (DIRECT, DIRECT, 1, 1), (RING, RING, 2, 0),
+    (TWO, RING, 2, 1), (RING, RING, 2, 0), (TWO, RING, 2, 1),
 )
 MESH_ID = pl.DeviceIdType.MESH
 F32 = jnp.float32
@@ -25,28 +25,25 @@
 BF16 = jnp.bfloat16
 
 PROGRAM = (
-    (5, None, 0), (0, None, 0), (1, None, 0), (2, None, 0), (3, None, 0), (10, None, 0), (6, None, 0), (4, None, 0),
-    (7, None, 0), (9, None, 0), (5, None, 1), (3, None, 1), (6, None, 1), (0, None, 1), (10, None, 1), (8, None, 0),
-    (1, None, 1), (5, None, 2), (2, None, 1), (3, None, 2), (3, 0, 0), (3, 1, 0), (8, None, 1), (4, None, 1),
-    (7, None, 1), (9, None, 1), (0, None, 2), (0, 0, 0), (0, 1, 0), (6, None, 2), (5, None, 3), (5, 0, 0),
-    (5, 1, 0), (10, None, 2), (1, None, 2), (1, 0, 0), (1, 1, 0), (2, None, 2), (3, 0, 1), (4, None, 2),
-    (8, None, 2), (3, 1, 1), (7, None, 2), (9, None, 2), (6, None, 3), (0, 0, 1), (1, 0, 1), (5, 0, 1),
-    (11, None, 0), (5, 1, 1), (0, 1, 1), (10, None, 3), (1, 1, 1), (4, None, 3), (4, 0, 0), (4, 1, 0), (3, 0, 2),
-    (2, None, 3), (2, 0, 0), (2, 1, 0), (9, None, 3), (3, 1, 2), (7, None, 3), (6, None, 4), (0, 1, 2), (5, 0, 2),
-    (0, 0, 2), (1, 1, 2), (1, 0, 2), ("keys", 0), (5, 1, 2), ("keys", 1), (11, None, 1), ("keys", 2), (10, None, 4),
-    ("keys", 3), (2, 0, 1), (3, 0, 3), (8, 0, 0), (4, 0, 1), (3, 1, 3), (8, 1, 0), (6, None, 5), (6, 0, 0),
-    (2, 1, 1), (9, None, 4), (5, 0, 3), (4, 1, 1), (6, 1, 0), (7, None, 4), (7, 0, 0), (7, 1, 0), (11, None, 2),
-    (11, 0, 0), (3, 0, 4), (5, 1, 3), (11, 1, 0), (10, None, 5), (2, 0, 2), (4, 0, 2), (8, 0, 1), (2, 1, 2),
-    (3, 1, 4), ("values", 0), ("values", 1), ("values", 2), (5, 0, 4), ("values", 3), (6, 0, 1), (9, 0, 0),
-    ("delta",), (8, 1, 1), (4, 1, 2), (7, 0, 1), (10, 0, 0), (11, 0, 1), (5, 1, 4), ("q", 0, 0), ("q", 0, 1),
-    (6, 1, 1), (9, 1, 0), (7, 1, 1), (10, 1, 0), ("q", 0, 2), ("q", 0, 3), (11, 1, 1), ("local", 0, 0),
-    ("local", 0, 1), (6, 0, 2), (8, 0, 2), ("rows",), (8, 1, 2), (9, 0, 1), (11, 0, 2), (6, 1, 2), (7, 0, 2),
-    (11, 1, 2), (8, 0, 3), (9, 1, 1), (10, 0, 1), (7, 1, 2), ("q", 1, 0), ("q", 1, 1), (8, 1, 3), ("q", 1, 2),
-    ("q", 1, 3), ("local", 1, 0), ("local", 1, 1), (11, 0, 3), (10, 1, 1), ("memory",), (8, 0, 4), (11, 1, 3),
-    ("finish", 0, 0), ("finish", 0, 1), ("finish", 1, 0), ("finish", 1, 1), (9, 0, 2), (8, 1, 4), (10, 0, 2),
-    (9, 1, 2), ("q", 2, 0), ("q", 2, 1), ("q", 2, 2), (11, 0, 4), ("q", 2, 3), ("local", 2, 0), (11, 1, 4),
-    ("finish", 2, 0), ("local", 2, 1), ("finish", 2, 1), (10, 1, 2), ("q", 3, 0), ("q", 3, 1), ("q", 3, 2),
-    ("q", 3, 3), ("local", 3, 0), ("finish", 3, 0), ("local", 3, 1), ("finish", 3, 1),
+    (3, None, 0), (0, None, 0), (1, None, 0), (2, None, 0), (4, None, 0), (5, None, 0), (6, None, 0), (8, None, 0),
+    (10, None, 0), (3, None, 1), (2, None, 1), (9, None, 0), (11, None, 0), (7, None, 0), (0, None, 1),
+    (6, None, 1), (1, None, 1), (3, None, 2), (4, None, 1), (5, None, 1), (8, None, 1), (10, None, 1), (7, None, 1),
+    (2, None, 2), (2, 0, 0), (9, None, 1), (6, None, 2), (11, None, 1), (4, None, 2), (5, None, 2), (8, None, 2),
+    (10, None, 2), (0, None, 2), (0, 0, 0), (0, 1, 0), (3, None, 3), (3, 0, 0), (1, None, 2), (1, 0, 0), (1, 1, 0),
+    (6, None, 3), (7, None, 2), (2, 0, 1), (9, None, 2), (5, None, 3), (4, None, 3), (11, None, 2), (8, None, 3),
+    (10, None, 3), (0, 0, 1), (1, 0, 1), (3, 0, 1), (0, 1, 1), (8, None, 4), (10, None, 4), (1, 1, 1), (2, 0, 2),
+    (5, None, 4), (5, 0, 0), (5, 1, 0), (9, None, 3), (4, None, 4), (4, 0, 0), (4, 1, 0), (11, None, 3), (3, 0, 2),
+    (0, 0, 2), (1, 0, 2), (0, 1, 2), (8, None, 5), (2, 0, 3), (6, 0, 0), (1, 1, 2), ("keys", 0), (10, None, 5),
+    ("keys", 1), ("keys", 2), ("keys", 3), (3, 0, 3), (7, 0, 0), (5, 0, 1), (4, 0, 1), (2, 0, 4), (10, None, 6),
+    (10, 0, 0), (4, 1, 1), (5, 1, 1), (10, 1, 0), (8, None, 6), (8, 0, 0), (8, 1, 0), (9, None, 4), (9, 0, 0),
+    (11, None, 4), (11, 0, 0), (3, 0, 4), ("values", 0), ("values", 1), (6, 0, 1), ("values", 2), ("values", 3),
+    (4, 0, 2), ("delta",), (5, 0, 2), (7, 0, 1), (4, 1, 2), (10, 0, 1), (11, 1, 0), ("q", 3, 0), (6, 0, 2),
+    (5, 1, 2), ("q", 0, 0), (8, 0, 1), (9, 1, 0), ("q", 0, 1), ("q", 0, 2), ("q", 0, 3), ("q", 2, 0), ("local", 0),
+    (10, 1, 1), (8, 1, 1), (7, 0, 2), (6, 0, 3), (11, 0, 1), (9, 0, 1), (10, 0, 2), (7, 0, 3), (8, 0, 2),
+    (11, 1, 1), ("q", 3, 1), ("q", 3, 2), ("rows",), (6, 0, 4), (10, 1, 2), (9, 1, 1), ("q", 2, 1), (11, 0, 2),
+    ("q", 2, 2), (7, 0, 4), ("q", 1, 0), ("q", 1, 1), ("q", 1, 2), ("q", 1, 3), (8, 1, 2), (11, 1, 2), ("q", 3, 3),
+    (9, 0, 2), ("local", 1), ("local", 3), (9, 1, 2), ("q", 2, 3), ("local", 2), ("memory",), ("finish", 0),
+    ("finish", 1), ("finish", 2), ("finish", 3),
 )
 
 
@@ -179,7 +176,7 @@
             )
         return made
 
-    sent = []
+    sent, flying = [], {}
 
     def tick(ch, sub, number):
         thread = (ch, sub)
@@ -196,12 +193,24 @@
                 one.wait_recv()
             for two in leaving:
                 two.start()
-        sent.extend(leaving)
+        for one in flying.pop(thread, ()):
+            one.wait_send()
+        flying[thread] = leaving
 
     def project(pair, i, dst):
         ch = 2 * pair
-        b = jnp.concatenate([w[ch, i].reshape(1024, HEAD), w[ch + 1, i].reshape(1024, HEAD)], axis=1)
-        a = tok[:, :, i * 1024 : (i + 1) * 1024].reshape(2 * SEG, 1024)
+        last = {ORDERS[ch][2], ORDERS[ch + 1][2]}
+        if last == {"x"}:
+            at = lax.rem(x + (0, 1, 3, 2)[i], 4)
+            b = [w[ch + e, :, at].reshape(1024, HEAD) for e in range(2)]
+            a = [tok[:, :, pl.ds(pl.multiple_of(k * 1024 + at * 256, 256), 256)] for k in range(4)]
+            a = jnp.concatenate(a, axis=2)
+        else:
+            at = lax.rem(y + (0, 1, 3, 2)[i], 4) if last == {"y"} else i
+            b = [w[ch + e, at].reshape(1024, HEAD) for e in range(2)]
+            a = tok[:, :, pl.ds(pl.multiple_of(at * 1024, 1024), 1024)]
+        a = a.reshape(2 * SEG, 1024)
+        b = jnp.concatenate(b, axis=1)
         r = jnp.dot(a, b, preferred_element_type=F32)
         if i:
             r += acc[pair]
@@ -280,19 +289,19 @@
     def stacked(j, s, rows):
         return jnp.concatenate([qbuf[j, s, rows, 0:HEAD], qbuf[j, s, rows, HEAD:]], axis=0)
 
-    def attend(j, second):
-        s = c if second else 1 - c
+    def attend(j):
         kcols = slice(j // 2 * HEAD, (j // 2 + 1) * HEAD)
         gates = sides(j)
-        valid = meta[s, 0:1, :]
-        for r in range(2):
-            nk = (r + 1) * HEAD
-            rows = slice(r * HEAD, (r + 1) * HEAD)
-            keys = kbuf[s, 0:nk, kcols]
-            vals = jnp.concatenate([vbuf[s, 0:nk, kcols], ones[0:nk]], axis=1)
-            scores = lax.dot_general(
-                stacked(j, s, rows), keys, (((1,), (1,)), ((), ())), preferred_element_type=F32
+        blocks = [(s, r, (r + 1) * HEAD, slice(r * HEAD, (r + 1) * HEAD)) for r in (1, 0) for s in range(2)]
+        scores = [
+            lax.dot_general(
+                stacked(j, s, rows), kbuf[s, 0:nk, kcols], (((1,), (1,)), ((), ())), preferred_element_type=F32
             )
+            for s, r, nk, rows in blocks
+        ]
+        expo = []
+        for (s, r, nk, rows), score in zip(blocks, scores):
+            valid = meta[s, 0:1, :]
             irow = lax.broadcasted_iota(jnp.int32, (HEAD, nk), 0) + r * HEAD
             jcol = lax.broadcasted_iota(jnp.int32, (HEAD, nk), 1)
             wide = valid if r == 0 else jnp.concatenate([valid, valid], axis=1)
@@ -301,14 +310,20 @@
                 lower = jnp.concatenate([meta[s, 1:2, :], jnp.ones((1, HEAD), jnp.int32)], axis=1)
                 allowed = allowed & (lower > 0)
             allowed = jnp.concatenate([allowed, allowed], axis=0)
-            masked = jnp.where(allowed, scores, -1e30)
+            masked = jnp.where(allowed, score, -1e30)
             top = jnp.max(masked, axis=1, keepdims=True)
-            expo = jnp.exp2((masked - top) * (HEAD**-0.5 * LOG2E)).astype(BF16)
-            local = jnp.dot(expo, vals, preferred_element_type=F32)
-            local = local[:, 0:HEAD] / jnp.maximum(local[:, HEAD:], 1.0)
+            expo.append(jnp.exp2((masked - top) * (HEAD**-0.5 * LOG2E)).astype(BF16))
+        local = [
+            jnp.dot(
+                weights, jnp.concatenate([vbuf[s, 0:nk, kcols], ones[0:nk]], axis=1), preferred_element_type=F32
+            )
+            for (s, r, nk, rows), weights in zip(blocks, expo)
+        ]
+        for (s, r, nk, rows), one in zip(blocks, local):
+            one = one[:, 0:HEAD] / jnp.maximum(one[:, HEAD:], 1.0)
             for e in range(2):
                 half = slice(e * HEAD, (e + 1) * HEAD)
-                loc[j, s, rows, half] = (1.0 - gates[e]) * local[half]
+                loc[j, s, rows, half] = (1.0 - gates[e]) * one[half]
 
     def finish(j, second):
         s = c if second else 1 - c
@@ -364,9 +379,10 @@
         elif name == "memory":
             memory()
         elif name == "local":
-            attend(where[0], where[1])
+            attend(where[0])
         elif name == "finish":
-            finish(where[0], where[1])
+            finish(where[0], False)
+            finish(where[0], True)
         else:
             tick(name, *where)
 

time: 83.5 us -> 82.3 us (0.986)
  Pallas kernels: 81.7 us -> 80.5 us
    pallas_call x1, Pallas kernels: 81.7 us -> 80.5 us  [shards(): pl.pallas_call(functools.partial(body, dims), out_shape=pltpu.VMEM((SEG,...]
where the time goes in v4:
time: 82.3 us; the launch traced here: 82.1 us
  Pallas kernels  80.5 us (98%)
  local copies, waits for them, and re-layouts  0.97 us (1%)
    pallas_call x1, Pallas kernels, shards(): pl.pallas_call(functools.partial(body, dims), out_shape=pltpu.VMEM((SEG,...  80.5 us

profile of v4, /device:TPU:1, one launch (start us, length us, event | category | flops | bytes accessed | tf_op | source)
XLA Modules:
  0.0 82.1 jit_solution(922892239333667457)
XLA Ops:
  0.7 80.5 %shard_map.73 = bf16[256,2048]{1,0:T(8,128)(2,1)S(1)} custom-call(bf16[256,4096]{1,0:T(8,128)(2,1)} %bitcast.4, bf16[16,2048]{1,0:T(8,128)(2,1)} %wq_hbm.1, bf16[16,512]{1,0:T(8,128)(2,1)} %wk_hbm.1, bf16[16,512]{1,0:T(8,128)(2,1)} %wv_hbm.1, f32[16]{0:T(128)} %gate_ref.1, s32[2,2]{1,0:T(2,128)} %bitcast.5, s32[1,1]{1,0:T(1,128)S(6)} %copy.10.valid_ref), custom_call_target="tpu_custom_call" | custom-call | tf_op jit(solution)/shard_map/pallas_call | solution.py:408
  81.1 1.0 %copy.9 = bf16[1,256,2048]{2,1,0:T(8,128)(2,1)} copy(bf16[1,256,2048]{2,1,0:T(8,128)(2,1)S(1)} %bitcast.3) | data formatting | bytes 2097152

commit v5 on v4

--- a/solution.py
+++ b/solution.py
@@ -289,10 +289,10 @@
     def stacked(j, s, rows):
         return jnp.concatenate([qbuf[j, s, rows, 0:HEAD], qbuf[j, s, rows, HEAD:]], axis=0)
 
-    def attend(j):
+    def attend(j, segments):
         kcols = slice(j // 2 * HEAD, (j // 2 + 1) * HEAD)
         gates = sides(j)
-        blocks = [(s, r, (r + 1) * HEAD, slice(r * HEAD, (r + 1) * HEAD)) for r in (1, 0) for s in range(2)]
+        blocks = [(s, r, (r + 1) * HEAD, slice(r * HEAD, (r + 1) * HEAD)) for r in (1, 0) for s in segments]
         scores = [
             lax.dot_general(
                 stacked(j, s, rows), kbuf[s, 0:nk, kcols], (((1,), (1,)), ((), ())), preferred_element_type=F32
@@ -352,15 +352,22 @@
             one.start()
             sent.append(one)
 
-    for here, back in zip(locals_, recvs_):
-        here.wait()
-        back.wait_recv()
-    for ch in range(NCH):
+    settled = set()
+
+    def settle(ch):
+        span = min(ch // 2, 2)
+        if span not in settled:
+            settled.add(span)
+            locals_[span].wait()
+            recvs_[span].wait_recv()
         w[ch, y, x, :, z] = wst[:, :, ch * HEAD : (ch + 1) * HEAD]
-    meta_copy.start()
-    tok_copy.start()
-    tok_here.start()
-    for name, *where in PROGRAM:
+
+    last_pair = [where[0] for name, *where in PROGRAM if name == "local"][-1]
+    for turn, (name, *where) in enumerate(PROGRAM):
+        if turn == 24:
+            meta_copy.start()
+            tok_copy.start()
+            tok_here.start()
         if name == "keys":
             if where[0] == 0:
                 tok_here.wait()
@@ -379,12 +386,18 @@
         elif name == "memory":
             memory()
         elif name == "local":
-            attend(where[0])
+            attend(where[0], (1 - c,) if where[0] == last_pair else (0, 1))
         elif name == "finish":
             finish(where[0], False)
-            finish(where[0], True)
+            if where[0] != last_pair:
+                finish(where[0], True)
         else:
+            if where == [None, 0]:
+                settle(name)
             tick(name, *where)
+
+    attend(last_pair, (c,))
+    finish(last_pair, True)
 
     for j in range(4):
         arriving = out_ref.at[:, pl.ds(pl.multiple_of((1 - c) * 4 * CW + j * CW, CW), CW)]

time: 82.3 us -> 82.1 us (level)
  no operation moved by 1% of the time
where the time goes in v5:
time: 82.1 us; the launch traced here: 82 us
  Pallas kernels  80.3 us (98%)
  local copies, waits for them, and re-layouts  0.97 us (1%)
    pallas_call x1, Pallas kernels, shards(): pl.pallas_call(functools.partial(body, dims), out_shape=pltpu.VMEM((SEG,...  80.3 us

profile of v5, /device:TPU:1, one launch (start us, length us, event | category | flops | bytes accessed | tf_op | source)
XLA Modules:
  0.0 82.0 jit_solution(1605016033603777143)
XLA Ops:
  0.7 80.3 %shard_map.73 = bf16[256,2048]{1,0:T(8,128)(2,1)S(1)} custom-call(bf16[256,4096]{1,0:T(8,128)(2,1)} %bitcast.4, bf16[16,2048]{1,0:T(8,128)(2,1)} %wq_hbm.1, bf16[16,512]{1,0:T(8,128)(2,1)} %wk_hbm.1, bf16[16,512]{1,0:T(8,128)(2,1)} %wv_hbm.1, f32[16]{0:T(128)} %gate_ref.1, s32[2,2]{1,0:T(2,128)} %bitcast.5, s32[1,1]{1,0:T(1,128)S(6)} %copy.10.valid_ref), custom_call_target="tpu_custom_call" | custom-call | tf_op jit(solution)/shard_map/pallas_call | solution.py:421
  81.0 1.0 %copy.9 = bf16[1,256,2048]{2,1,0:T(8,128)(2,1)} copy(bf16[1,256,2048]{2,1,0:T(8,128)(2,1)S(1)} %bitcast.3) | data formatting | bytes 2097152

commit v6 on v5

--- a/solution.py
+++ b/solution.py
@@ -106,7 +106,7 @@
         recvs_.append(back)
 
     row8 = lax.broadcasted_iota(jnp.int32, (8, HEAD), 0)
-    meta[c] = jnp.where(row8 == 0, valid_ref[0, 0], mask_ref[1, 0])
+    meta[c] = jnp.where(row8 == 0, valid_ref[0], mask_ref[1, 0])
     meta_copy = pltpu.make_async_remote_copy(
         meta.at[c], meta.at[c], csem_s.at[3], csem_r.at[3], device_id=sibling, device_id_type=MESH_ID
     )
@@ -451,7 +451,7 @@
             compiler_params=pltpu.CompilerParams(
                 collective_id=0, has_side_effects=True, vmem_limit_bytes=56 * 1024 * 1024
             ),
-        )(tokens[0], w_query, w_key, value_weight, gate_bias, block_mask[0, 0], valid_len)
+        )(tokens[0], w_query, w_key, value_weight, gate_bias, block_mask[0, 0], valid_len.reshape(1))
         return out[None]
 
     in_specs = (

time: 82.1 us -> 82.1 us (level)
  no operation moved by 1% of the time
where the time goes in v6:
time: 82.1 us; the launch traced here: 82 us
  Pallas kernels  80.3 us (98%)
  local copies, waits for them, and re-layouts  0.97 us (1%)
    pallas_call x1, Pallas kernels, shards(): pl.pallas_call(functools.partial(body, dims), out_shape=pltpu.VMEM((SEG,...  80.3 us

profile of v6, /device:TPU:1, one launch (start us, length us, event | category | flops | bytes accessed | tf_op | source)
XLA Modules:
  0.0 82.0 jit_solution(1605016033603777143)
XLA Ops:
  0.7 80.3 %shard_map.73 = bf16[256,2048]{1,0:T(8,128)(2,1)S(1)} custom-call(bf16[256,4096]{1,0:T(8,128)(2,1)} %bitcast.6, bf16[16,2048]{1,0:T(8,128)(2,1)} %wq_hbm.1, bf16[16,512]{1,0:T(8,128)(2,1)} %wk_hbm.1, bf16[16,512]{1,0:T(8,128)(2,1)} %wv_hbm.1, f32[16]{0:T(128)} %gate_ref.1, s32[2,2]{1,0:T(2,128)} %bitcast.7, s32[1]{0:T(128)} %bitcast.4.valid_ref), custom_call_target="tpu_custom_call" | custom-call | tf_op jit(solution)/shard_map/pallas_call | solution.py:421
  81.0 1.0 %copy.9 = bf16[1,256,2048]{2,1,0:T(8,128)(2,1)} copy(bf16[1,256,2048]{2,1,0:T(8,128)(2,1)S(1)} %bitcast.5) | data formatting | bytes 2097152
